TPU v7x, 32 devices: a whole 2x2x4 slice. The times are simulated.
32 devices in a mesh: dp: 8 (over y, x, core), tensor: 4 (over z).
Axes of the slice: x: 2, y: 2, z: 4, core: 2. Of those that a mesh axis runs over, the one named last changes fastest.
Arguments:
- block_input: bfloat16 [4096, 768], P(('dp', 'tensor')), may hold values from -6 to 6
- seq_lengths: int32 [8, 4], P('dp'), may hold values from 0 to 512, as said below
- w_qkv: bfloat16 [768, 2304], P(None, 'tensor'), may hold values from -3 to 3
- b_query: float32 [768], P('tensor'), may hold values from -3 to 3
- b_value: float32 [768], P('tensor'), may hold values from -3 to 3
- w_out: bfloat16 [768, 768], P('tensor'), may hold values from -1 to 1
- b_out: float32 [768], replicated, may hold values from -3 to 3
- w_up: bfloat16 [768, 3072], P(None, 'tensor'), may hold values from -0.21875 to 0.21875
- b_up: float32 [3072], P('tensor'), may hold values from -3 to 3
- w_down: bfloat16 [3072, 768], P('tensor'), may hold values from -0.109375 to 0.109375
- b_down: float32 [768], replicated, may hold values from -3 to 3
- first_norm_gain: float32 [768], replicated, may hold values from 0.1 to 1.9
- first_norm_bias: float32 [768], replicated, may hold values from -2 to 2
- second_norm_gain: float32 [768], replicated, may hold values from 0.1 to 1.9
- second_norm_bias: float32 [768], replicated, may hold values from -2 to 2
- cotangent: bfloat16 [4096, 768], P(('dp', 'tensor')), may hold values from -6 to 6
Outputs:
- block_output: bfloat16 [4096, 768], P(('dp', 'tensor'))
- grad_input: float32 [4096, 768], P(('dp', 'tensor'))
- grad_w_qkv: float32 [768, 2304], P(None, 'tensor')
- grad_b_query: float32 [768], P('tensor')
- grad_b_value: float32 [768], P('tensor')
- grad_w_out: float32 [768, 768], P('tensor')
- grad_b_out: float32 [768], replicated
- grad_w_up: float32 [768, 3072], P(None, 'tensor')
- grad_b_up: float32 [3072], P('tensor')
- grad_w_down: float32 [3072, 768], P('tensor')
- grad_b_down: float32 [768], replicated
- first_norm_gain_gradient: float32 [768], replicated
- first_norm_bias_gradient: float32 [768], replicated
- second_norm_gain_gradient: float32 [768], replicated
- second_norm_bias_gradient: float32 [768], replicated
Inputs may be any that keep to these rules, and one draw needn't show every extreme that they name: `seq_lengths`: row g lists the lengths of the sequences packed one after another from slot 0 into the 512 slots of group g; a row sums to at most 512, some entries may be 0, and some row fills all its slots.
All inputs are finite; a program needn't handle non-finite values.
Results may differ from a plain program's by a relative error of at most 0.012.
Values may be sent and summed in bfloat16 or wider, within the bound.
No kernel may reach another device: no remote copies, remote signals or barrier semaphores. Data moves between devices by JAX's collectives and lax.ppermute only.
A program may use at most 64 MiB of HBM per device.

v0:
```python
import math

import jax
import jax.numpy as jnp
from jax import lax
from jax.sharding import PartitionSpec as P

HD = 64


GELU_COEF = 0.7978845608028654
GELU_CUBE = 0.044715
NORM_EPS = 1e-05


def gelu_tanh(values):
    inner_arg = GELU_COEF * (values + GELU_CUBE * values * values * values)
    return 0.5 * values * (1.0 + jnp.tanh(inner_arg))


def gelu_slope(values):
    tangent = jnp.tanh(GELU_COEF * (values + GELU_CUBE * values * values * values))
    return 0.5 * (1.0 + tangent) + 0.5 * values * (1.0 - tangent * tangent) * GELU_COEF * (
        1.0 + 3.0 * GELU_CUBE * values * values
    )


def layer_normalize(values, gain, bias_vec):
    row_mean = jnp.mean(values, axis=-1, keepdims=True)
    centred = values - row_mean
    rstd_row = lax.rsqrt(jnp.mean(centred * centred, axis=-1, keepdims=True) + NORM_EPS)
    normed = centred * rstd_row
    return ((normed * gain + bias_vec).astype(jnp.bfloat16), normed, rstd_row)


def layer_normalize_backward(grad_normed, normed, rstd_row, gain):
    scaled = grad_normed * gain
    inner_mean = jnp.mean(scaled * normed, axis=-1, keepdims=True)
    grad_rows = rstd_row * (scaled - jnp.mean(scaled, axis=-1, keepdims=True) - normed * inner_mean)
    return (grad_rows, jnp.sum(grad_normed * normed, axis=0), jnp.sum(grad_normed, axis=0))


def contract_rows(left, right):
    return lax.dot_general(
        left, right, (((0,), (0,)), ((), ())), preferred_element_type=jnp.float32
    )


def times_transposed(left, right):
    return lax.dot_general(
        left, right, (((1,), (1,)), ((), ())), preferred_element_type=jnp.float32
    )


def block_scores(query_block, key_rows, segment, slot_ids):
    scale = 1.0 / math.sqrt(HD)
    allowed = (segment[:, None] == segment[None, :]) & (slot_ids[None, :] <= slot_ids[:, None])
    scores = (
        jnp.einsum("qhe,khe->hqk", query_block, key_rows, preferred_element_type=jnp.float32)
        * scale
    )
    return jnp.where(allowed[None, :, :], scores, -jnp.inf)


def attend_forward(queries, key_rows, values, segment, slot_ids):
    scores = block_scores(queries, key_rows, segment, slot_ids)
    row_top = jnp.max(scores, axis=-1, keepdims=True)
    log_total = row_top + jnp.log(jnp.sum(jnp.exp(scores - row_top), axis=-1, keepdims=True))
    prob_bf = jnp.exp(scores - log_total).astype(jnp.bfloat16)
    outputs = jnp.einsum(
        "hqk,khe->qhe", prob_bf, values, preferred_element_type=jnp.float32
    ).astype(jnp.bfloat16)
    totals = [log_total]
    return (outputs, totals)


def attend_backward(queries, key_rows, values, attended, grad_att, totals, segment, slot_ids):
    scale = 1.0 / math.sqrt(HD)
    scores = block_scores(queries, key_rows, segment, slot_ids)
    prob_full = jnp.exp(scores - totals[0])
    prob_bf = prob_full.astype(jnp.bfloat16)
    grad_values = jnp.einsum("hqk,qhe->khe", prob_bf, grad_att, preferred_element_type=jnp.float32)
    grad_probs = jnp.einsum("qhe,khe->hqk", grad_att, values, preferred_element_type=jnp.float32)
    row_delta = jnp.sum(grad_att.astype(jnp.float32) * attended.astype(jnp.float32), axis=-1)
    grad_scores = (prob_full * (grad_probs - jnp.transpose(row_delta)[:, :, None]) * scale).astype(
        jnp.bfloat16
    )
    grad_query_list = jnp.einsum(
        "hqk,khe->qhe", grad_scores, key_rows, preferred_element_type=jnp.float32
    )
    grad_keys = jnp.einsum("hqk,qhe->khe", grad_scores, queries, preferred_element_type=jnp.float32)
    return (grad_query_list, grad_keys, grad_values)


def local(
    block_input,
    seq_lengths,
    w_qkv,
    b_query,
    b_value,
    w_out,
    b_out,
    w_up,
    b_up,
    w_down,
    b_down,
    first_norm_gain,
    first_norm_bias,
    second_norm_gain,
    second_norm_bias,
    cotangent,
):
    own_rows = block_input.shape[0]
    group_rows = own_rows * lax.axis_size("tensor")
    heads_here = w_out.shape[0] // HD
    slot_ids = jnp.arange(group_rows, dtype=jnp.int32)
    seq_ends = jnp.cumsum(seq_lengths[0])
    segment = jnp.sum((slot_ids[:, None] >= seq_ends[None, :]).astype(jnp.int32), axis=1)
    valid_slot = (slot_ids < seq_ends[-1]).astype(jnp.float32)
    first_slot = lax.axis_index("tensor") * own_rows
    valid_col = lax.dynamic_slice_in_dim(valid_slot, first_slot, own_rows, 0)[:, None]
    input_as_float = block_input.astype(jnp.float32)
    first_normalized, first_standardized, first_inverse_deviation = layer_normalize(
        input_as_float, first_norm_gain, first_norm_bias
    )
    rows_one = lax.all_gather(first_normalized, "tensor", axis=0, tiled=True)
    joined_rows = jnp.dot(rows_one, w_qkv, preferred_element_type=jnp.float32).reshape(
        group_rows, heads_here, 3, HD
    )
    queries = (joined_rows[:, :, 0] + b_query.reshape(heads_here, HD)).astype(jnp.bfloat16)
    key_rows = joined_rows[:, :, 1].astype(jnp.bfloat16)
    values = (joined_rows[:, :, 2] + b_value.reshape(heads_here, HD)).astype(jnp.bfloat16)
    attended, totals = attend_forward(queries, key_rows, values, segment, slot_ids)
    attended_flat = attended.reshape(group_rows, heads_here * HD)
    attn_part = lax.psum_scatter(
        jnp.dot(attended_flat, w_out, preferred_element_type=jnp.float32),
        "tensor",
        scatter_dimension=0,
        tiled=True,
    )
    residual_stream_rows = input_as_float + attn_part + b_out
    second_normalized, second_standardized, second_inverse_deviation = layer_normalize(
        residual_stream_rows, second_norm_gain, second_norm_bias
    )
    rows_two = lax.all_gather(second_normalized, "tensor", axis=0, tiled=True)
    pre_act = jnp.dot(rows_two, w_up, preferred_element_type=jnp.float32) + b_up
    activation = gelu_tanh(pre_act).astype(jnp.bfloat16)
    mlp_part = lax.psum_scatter(
        jnp.dot(activation, w_down, preferred_element_type=jnp.float32),
        "tensor",
        scatter_dimension=0,
        tiled=True,
    )
    final_rows = residual_stream_rows + mlp_part + b_down
    block_output = (final_rows * valid_col).astype(jnp.bfloat16)
    grad_final = cotangent.astype(jnp.float32) * valid_col
    grad_final_bf = grad_final.astype(jnp.bfloat16)
    final_all = lax.all_gather(grad_final_bf, "tensor", axis=0, tiled=True)
    grad_w_down = contract_rows(activation, final_all)
    grad_b_down = jnp.sum(grad_final, axis=0)
    grad_pre = times_transposed(final_all, w_down) * gelu_slope(pre_act)
    grad_pre_bf = grad_pre.astype(jnp.bfloat16)
    grad_w_up = contract_rows(rows_two, grad_pre_bf)
    grad_b_up = jnp.sum(grad_pre, axis=0)
    second_normalized_gradient = lax.psum_scatter(
        times_transposed(grad_pre_bf, w_up), "tensor", scatter_dimension=0, tiled=True
    )
    second_norm_backward, second_norm_gain_gradient, second_norm_bias_gradient = (
        layer_normalize_backward(
            second_normalized_gradient,
            second_standardized,
            second_inverse_deviation,
            second_norm_gain,
        )
    )
    grad_residual = grad_final + second_norm_backward
    grad_residual_bf = grad_residual.astype(jnp.bfloat16)
    residual_all = lax.all_gather(grad_residual_bf, "tensor", axis=0, tiled=True)
    grad_w_out = contract_rows(attended_flat, residual_all)
    grad_b_out = jnp.sum(grad_residual, axis=0)
    grad_att = (
        times_transposed(residual_all, w_out)
        .astype(jnp.bfloat16)
        .reshape(group_rows, heads_here, HD)
    )
    grad_queries, grad_keys, grad_values = attend_backward(
        queries, key_rows, values, attended, grad_att, totals, segment, slot_ids
    )
    grad_b_query = jnp.sum(grad_queries, axis=0).reshape(heads_here * HD)
    grad_b_value = jnp.sum(grad_values, axis=0).reshape(heads_here * HD)
    grad_joined = jnp.stack(
        [
            grad_queries.astype(jnp.bfloat16),
            grad_keys.astype(jnp.bfloat16),
            grad_values.astype(jnp.bfloat16),
        ],
        axis=2,
    ).reshape(group_rows, heads_here * 3 * HD)
    grad_w_qkv = contract_rows(rows_one, grad_joined)
    first_normalized_gradient = lax.psum_scatter(
        times_transposed(grad_joined, w_qkv), "tensor", scatter_dimension=0, tiled=True
    )
    first_norm_backward, first_norm_gain_gradient, first_norm_bias_gradient = (
        layer_normalize_backward(
            first_normalized_gradient, first_standardized, first_inverse_deviation, first_norm_gain
        )
    )
    grad_input = grad_residual + first_norm_backward
    grad_w_qkv, grad_b_query, grad_b_value, grad_w_out, grad_w_up, grad_b_up, grad_w_down = (
        lax.psum(
            (grad_w_qkv, grad_b_query, grad_b_value, grad_w_out, grad_w_up, grad_b_up, grad_w_down),
            "dp",
        )
    )
    (
        first_norm_gain_gradient,
        first_norm_bias_gradient,
        second_norm_gain_gradient,
        second_norm_bias_gradient,
        grad_b_out,
        grad_b_down,
    ) = lax.psum(
        (
            first_norm_gain_gradient,
            first_norm_bias_gradient,
            second_norm_gain_gradient,
            second_norm_bias_gradient,
            grad_b_out,
            grad_b_down,
        ),
        ("dp", "tensor"),
    )
    return (
        block_output,
        grad_input,
        grad_w_qkv,
        grad_b_query,
        grad_b_value,
        grad_w_out,
        grad_b_out,
        grad_w_up,
        grad_b_up,
        grad_w_down,
        grad_b_down,
        first_norm_gain_gradient,
        first_norm_bias_gradient,
        second_norm_gain_gradient,
        second_norm_bias_gradient,
    )


def solution(mesh):
    placed = (
        P(("dp", "tensor"), None),
        P("dp", None),
        P(None, "tensor"),
        P("tensor"),
        P("tensor"),
        P("tensor", None),
        P(),
        P(None, "tensor"),
        P("tensor"),
        P("tensor", None),
        P(),
        P(),
        P(),
        P(),
        P(),
        P(("dp", "tensor"), None),
    )
    return jax.shard_map(
        local,
        mesh=mesh,
        in_specs=placed,
        out_specs=(
            P(("dp", "tensor"), None),
            P(("dp", "tensor"), None),
            P(None, "tensor"),
            P("tensor"),
            P("tensor"),
            P("tensor", None),
            P(),
            P(None, "tensor"),
            P("tensor"),
            P("tensor", None),
            P(),
            P(),
            P(),
            P(),
            P(),
        ),
        check_vma=False,
    )
```

profile of v0, /device:TPU:0, one launch (start us, length us, event | category | flops | bytes accessed | tf_op | source)
XLA Modules:
  0.0 380.8 jit_solution(3234579037893702764)
XLA Ops:
  11.2 21.3 %all_gather.12 = bf16[512,768]{1,0:T(8,128)(2,1)S(1)} all-gather(bf16[128,768]{1,0:T(8,128)(2,1)S(1)} %fusion.17), channel_id=1, replica_groups=mesh['dp'=8,'tensor'=4] {'tensor'}, dimensions={0}, use_global_device_ids=true | all-gather | bytes 983040 | tf_op jit(solution)/shard_map/all_gather | solution.py:126
  35.6 1.9 fusion.1
  40.1 1.6 fusion.58
  43.2 26.8 %all_gather.14 = bf16[512,768]{1,0:T(8,128)(2,1)} all-gather(bf16[128,768]{1,0:T(8,128)(2,1)S(1)} %fusion.34), channel_id=1, replica_groups=mesh['dp'=8,'tensor'=4] {'tensor'}, dimensions={0}, use_global_device_ids=true | all-gather | bytes 983040 | tf_op jit(solution)/shard_map/all_gather | solution.py:158
  70.0 15.3 %reduce-scatter.5.cloned.1.call-done = f32[128,768]{1,0:T(8,128)} async-done(((f32[512,768]{1,0:T(8,128)}), f32[128,768]{1,0:T(8,128)}) %reduce-scatter.5.cloned.1.call-update) | async-done | bytes 393232 | tf_op jit(solution)/shard_map/reduce_scatter | solution.py:135
  86.9 18.7 %all_gather.13 = bf16[512,768]{1,0:T(8,128)(2,1)S(1)} all-gather(bf16[128,768]{1,0:T(8,128)(2,1)S(1)} %add_convert_fusion), channel_id=1, replica_groups=mesh['dp'=8,'tensor'=4] {'tensor'}, dimensions={0}, use_global_device_ids=true | all-gather | bytes 983040 | tf_op jit(solution)/shard_map/all_gather | solution.py:145
  107.6 2.0 fusion.54
  110.7 2.0 fusion.31
  112.7 3.6 fusion.47
  116.4 31.1 %reduce-scatter.9.cloned.1.call-done = f32[128,768]{1,0:T(8,128)} async-done(((f32[512,768]{1,0:T(8,128)}), f32[128,768]{1,0:T(8,128)}) %reduce-scatter.9.cloned.1.call-update) | async-done | bytes 393232 | tf_op jit(solution)/shard_map/reduce_scatter | solution.py:165
  148.8 36.0 %reduce-scatter.7.cloned.1.call-done = f32[128,768]{1,0:T(8,128)} async-done(((f32[512,768]{1,0:T(8,128)}), f32[128,768]{1,0:T(8,128)}) %reduce-scatter.7.cloned.1.call-update) | async-done | bytes 393232 | tf_op jit(solution)/shard_map/reduce_scatter | solution.py:148
  184.7 2.2 fusion.48
  187.7 18.1 %all_gather.15 = bf16[512,768]{1,0:T(8,128)(2,1)S(1)} all-gather(bf16[128,768]{1,0:T(8,128)(2,1)S(1)} %convert_element_type.93), channel_id=1, replica_groups=mesh['dp'=8,'tensor'=4] {'tensor'}, dimensions={0}, use_global_device_ids=true | all-gather | bytes 983040 | tf_op jit(solution)/shard_map/all_gather | solution.py:178
  209.3 2.1 fusion.52
  212.6 2.0 fusion.59
  214.7 3.7 fusion.29
  218.4 2.3 fusion.46
  221.9 1.8 fusion.61
  224.6 13.1 %all-reduce.1 = (f32[192]{0:T(256)}, f32[192]{0:T(256)}, f32[768]{0:T(1024)}) all-reduce(f32[192]{0:T(256)S(1)} %reshape.163, f32[192]{0:T(256)S(1)} %reshape.164, f32[768]{0:T(1024)S(1)} %copy-done.36), channel_id=1, replica_groups=mesh['dp'=8,'tensor'=4] {'dp'}, use_global_device_ids=true, to_apply=%region_19.20 | all-reduce | flops 1152 | bytes 9216 | tf_op jit(solution)/shard_map/psum | solution.py:210
  237.6 11.9 %reduce-scatter.11.cloned.1.call-done = f32[128,768]{1,0:T(8,128)} async-done(((f32[512,768]{1,0:T(8,128)}), f32[128,768]{1,0:T(8,128)}) %reduce-scatter.11.cloned.1.call-update) | async-done | bytes 393232 | tf_op jit(solution)/shard_map/reduce_scatter | solution.py:200
  250.7 40.5 %all-reduce = (f32[768]{0:T(1024)}, f32[768]{0:T(1024)}, f32[768]{0:T(1024)}, f32[768]{0:T(1024)}, f32[768]{0:T(1024)}, /*index=5*/f32[768]{0:T(1024)}) all-reduce(f32[768]{0:T(1024)S(1)} %get-tuple-element.36, f32[768]{0:T(1024)S(1)} %get-tuple-element.47, ...), channel_id=1, replica_groups=mesh['dp'=8,'tensor'=4] {'dp','tensor'}, use_global_device_ids=true, to_apply=%region_24.25 | all-reduce | flops 4608 | bytes 36864 | tf_op jit(solution)/shard_map/psum | solution.py:222
  291.3 1.9 fusion.21
  293.2 73.4 %all-reduce.5.cloned.1.call-done = (f32[768,576]{0,1:T(8,128)}, f32[192,768]{1,0:T(8,128)}, f32[768,768]{1,0:T(8,128)}, f32[768,768]{1,0:T(8,128)}) async-done(((f32[768,576]{0,1:T(8,128)}, f32[192,768]{1,0:T(8,128)}, f32[768,768]{1,0:T(8,128)}, f32[768,768]{1,0:T(8,128)}), (f32[768,576]{0,1:T(8,128)}, f32[192,768]{1,0:T(8,128)}, f32[768,768]{1,0:T(8,128)}, ...) | async-done | bytes 7077904 | tf_op jit(solution)/shard_map/psum | solution.py:210
  366.6 2.9 copy.94
  (143 shorter events, 30.5 us)
Async XLA Ops:
  7.2 100.1 %copy-start = (bf16[768,768]{1,0:T(8,128)(2,1)S(1)}, bf16[768,768]{1,0:T(8,128)(2,1)}, u32[]{:S(2)}) copy-start(bf16[768,768]{1,0:T(8,128)(2,1)} %param.25) | copy-start | bytes 3538948
  7.2 78.1 %reduce-scatter.5.cloned.1.call-start = ((), (), s32[]{:S(2)}) async-start(), calls=%async_computation.4 | async-start | bytes 1966080 | tf_op jit(solution)/shard_map/reduce_scatter | solution.py:135
  7.2 25.3 %copy-start.6 = (bf16[768,576]{0,1:T(8,128)(2,1)S(1)}, bf16[768,576]{0,1:T(8,128)(2,1)}, u32[]{:S(2)}) copy-start(bf16[768,576]{0,1:T(8,128)(2,1)} %param.18) | copy-start | bytes 2654212
  33.2 5.0 %copy-start.4 = (f32[512,576]{0,1:T(8,128)}, f32[512,576]{0,1:T(8,128)S(1)}, u32[]{:S(2)}) copy-start(f32[512,576]{0,1:T(8,128)S(1)} %fusion.57) | copy-start | bytes 3538948
  40.1 167.1 %copy-start.15 = (bf16[3,64,512]{2,1,0:T(8,128)(2,1)}, bf16[3,64,512]{2,1,0:T(8,128)(2,1)S(1)}, u32[]{:S(2)}) copy-start(bf16[3,64,512]{2,1,0:T(8,128)(2,1)S(1)} %convolution_convert_fusion.1) | copy-start | bytes 589828
  41.7 43.6 %copy-start.3 = (bf16[128,768]{1,0:T(8,128)(2,1)S(1)}, bf16[128,768]{1,0:T(8,128)(2,1)}, u32[]{:S(2)}) copy-start(bf16[128,768]{1,0:T(8,128)(2,1)} %param.16) | copy-start | bytes 589828
  41.7 43.6 %copy-start.33 = (f32[768]{0:T(1024)S(1)}, f32[768]{0:T(1024)}, u32[]{:S(2)}) copy-start(f32[768]{0:T(1024)} %param.22) | copy-start | bytes 9220
  41.7 45.0 %copy-start.25 = (f32[768]{0:T(1024)S(1)}, f32[768]{0:T(1024)}, u32[]{:S(2)}) copy-start(f32[768]{0:T(1024)} %param.29) | copy-start | bytes 9220
  41.7 45.0 %copy-start.34 = (f32[768]{0:T(1024)S(1)}, f32[768]{0:T(1024)}, u32[]{:S(2)}) copy-start(f32[768]{0:T(1024)} %param.30) | copy-start | bytes 9220
  41.8 105.8 %reduce-scatter.9.cloned.1.call-start = ((), (), s32[]{:S(2)}) async-start(), calls=%async_computation.6 | async-start | bytes 1966080 | tf_op jit(solution)/shard_map/reduce_scatter | solution.py:165
  70.0 36.5 %copy-start.40 = (f32[768]{0:T(1024)S(1)}, f32[768]{0:T(1024)}, u32[]{:S(2)}) copy-start(f32[768]{0:T(1024)} %param.24) | copy-start | bytes 9220
  85.3 21.2 %copy-start.39 = (bf16[768,768]{1,0:T(8,128)(2,1)S(1)}, bf16[768,768]{1,0:T(8,128)(2,1)}, u32[]{:S(2)}) copy-start(bf16[768,768]{1,0:T(8,128)(2,1)} %param.23) | copy-start | bytes 3538948
  112.6 72.1 %reduce-scatter.7.cloned.1.call-start = ((), (), s32[]{:S(2)}) async-start(), calls=%async_computation.5 | async-start | bytes 1966080 | tf_op jit(solution)/shard_map/reduce_scatter | solution.py:148
  116.3 68.4 %copy-start.35 = (f32[768]{0:T(1024)S(1)}, f32[768]{0:T(1024)}, u32[]{:S(2)}) copy-start(f32[768]{0:T(1024)} %param.26) | copy-start | bytes 9220
  116.3 133.2 %reduce-scatter.11.cloned.1.call-start = ((), (), s32[]{:S(2)}) async-start(), calls=%async_computation.7 | async-start | bytes 1966080 | tf_op jit(solution)/shard_map/reduce_scatter | solution.py:200
  184.7 21.5 %copy-start.2 = (f32[3,512,512]{1,2,0:T(8,128)S(1)}, f32[3,512,512]{1,2,0:T(8,128)}, u32[]{:S(2)}) copy-start(f32[3,512,512]{1,2,0:T(8,128)} %copy-done.1) | copy-start | bytes 9437188
  186.9 19.3 %copy-start.14 = (pred[512,512]{0,1:T(8,128)(4,1)S(1)}, pred[512,512]{0,1:T(8,128)(4,1)}, u32[]{:S(2)}) copy-start(pred[512,512]{0,1:T(8,128)(4,1)} %fusion.9) | copy-start | bytes 786436
  214.6 152.0 %all-reduce.5.cloned.1.call-start = ((), (), s32[]{:S(2)}) async-start(), calls=%async_computation.8 | async-start | bytes 14155776 | tf_op jit(solution)/shard_map/psum | solution.py:210
  214.6 3.8 copy-start.20
  223.7 25.8 %copy-start.26 = (f32[768]{0:T(1024)S(1)}, f32[768]{0:T(1024)}, u32[]{:S(2)}) copy-start(f32[768]{0:T(1024)} %param.27) | copy-start | bytes 9220
  223.7 25.8 %copy-start.28 = (f32[128]{0:T(128)S(1)}, f32[128]{0:T(128)}, u32[]{:S(2)}) copy-start(f32[128]{0:T(128)} %copy-done.27) | copy-start | bytes 1540
  223.8 25.8 %copy-start.32 = (f32[128]{0:T(128)S(1)}, f32[128]{0:T(128)}, u32[]{:S(2)}) copy-start(f32[128]{0:T(128)} %copy-done.31) | copy-start | bytes 1540
  223.8 67.5 %copy-start.9 = (f32[128,768]{1,0:T(8,128)S(1)}, f32[128,768]{1,0:T(8,128)}, u32[]{:S(2)}) copy-start(f32[128,768]{1,0:T(8,128)} %copy-done.8) | copy-start | bytes 1179652
  366.6 3.8 copy-start.12
  (25 other events, 39.9 us)
Sparse Core Ops, SparseCore 0:
  41.8 43.3 reduce-scatter.4
  112.8 34.6 reduce-scatter.8
  150.4 34.2 reduce-scatter.6
  214.7 34.7 reduce-scatter.10
  254.2 112.3 all-reduce.4
where the time goes:
time: 382 us; the launch traced here: 381 us
  waiting for transfers between devices  168 us (44%)
  blocking collectives  138 us (36%)
  matrix products  30 us (8%)
  local copies, waits for them, and re-layouts  15.9 us (4%)
  other arithmetic  14.4 us (4%)
  between operations  14.2 us (4%)
    psum x1, waiting for transfers between devices, local(): lax.psum((grad_w_qkv, grad_b_query, grad_b_value, grad_w_out, grad_w_up,...  73.4 us
    psum x1, blocking collectives, local(): lax.psum((first_norm_gain_gradient, first_norm_bias_gradient, second_norm...  40.5 us
    reduce_scatter x1, waiting for transfers between devices, local(): lax.psum_scatter(jnp.dot(activation, w_down, preferred_element_type=jnp.f...  36 us
    reduce_scatter x1, waiting for transfers between devices, local(): lax.psum_scatter(times_transposed(grad_pre_bf, w_up), 'tensor', scatter_d...  31.1 us
    all_gather x1, blocking collectives, local(): final_all = lax.all_gather(grad_final_bf, 'tensor', axis=0, tiled=True)  26.8 us
    all_gather x1, blocking collectives, local(): rows_one = lax.all_gather(first_normalized, 'tensor', axis=0, tiled=True)  21.3 us
    all_gather x1, blocking collectives, local(): rows_two = lax.all_gather(second_normalized, 'tensor', axis=0, tiled=True)  18.7 us
    all_gather x1, blocking collectives, local(): lax.all_gather(grad_residual_bf, 'tensor', axis=0, tiled=True)  18.1 us
  transfers between devices with their start and end apart: 5, of which 5 were waited for; matrix products, arithmetic and copies ran while one was open for 5% of the time, Pallas kernels for 0%

commit v1 on v0

v1 whole, which is shorter than its diff:
```python
import math

import jax
import jax.numpy as jnp
from jax import lax
from jax.experimental import pallas as pl
from jax.experimental.pallas import tpu as pltpu
from jax.sharding import PartitionSpec as P


HD = 64
GELU_COEF = 0.7978845608028654
GELU_CUBE = 0.044715
NORM_EPS = 1e-05
SCALE = 1.0 / math.sqrt(HD)
BF = jnp.bfloat16
F32 = jnp.float32
VEC = 8


def dot(left, right, left_dim, right_dim):
    return lax.dot_general(
        left, right, (((left_dim,), (right_dim,)), ((), ())), preferred_element_type=F32
    )


def swap(x, axis, mask):
    n = lax.axis_size(axis)
    return lax.ppermute(x, axis, [(i, i ^ mask) for i in range(n)])


def z_size():
    return lax.axis_size("tensor")


def plane_size():
    return min(8, lax.axis_size("dp"))


def send_z(blocks):
    return [swap(blocks[m - 1], "tensor", m) for m in range(1, z_size())]


def gather_z(x):
    return send_z([x] * (z_size() - 1))


def send_plane(blocks):
    return [swap(blocks[k - 1], "dp", 2 * k) for k in range(1, plane_size() // 2)]


def gather_plane(x):
    mine = join([x] + send_plane([x] * (plane_size() // 2 - 1)))
    return mine, swap(mine, "dp", 1)


def beyond(x):
    mask = plane_size()
    while mask < lax.axis_size("dp"):
        x = x.astype(F32)
        x = x + swap(x, "dp", mask)
        mask *= 2
    return x


def shape(rows, cols, dtype):
    return jax.ShapeDtypeStruct((rows, cols), dtype)


def size_of(x):
    return x.size * x.dtype.itemsize


def grant(args, outs, scratch, room):
    total = sum(size_of(a) for a in args) + sum(size_of(o) for o in outs)
    total += sum(math.prod(s.shape) * jnp.dtype(s.dtype).itemsize for s in scratch)
    return pltpu.CompilerParams(vmem_limit_bytes=total + room)


def call(body, outs, args, *, flops=0, scratch=(), smem=0, room=1 << 20):
    given = [pl.BlockSpec(memory_space=pltpu.SMEM)] * smem
    given += [pl.BlockSpec(memory_space=pltpu.VMEM)] * (len(args) - smem)
    single = not isinstance(outs, (list, tuple))
    outs = [outs] if single else list(outs)
    cost = pl.CostEstimate(
        flops=flops,
        bytes_accessed=sum(size_of(a) for a in args) + sum(size_of(o) for o in outs),
        transcendentals=0,
    )
    result = pl.pallas_call(
        body,
        out_shape=outs,
        in_specs=given,
        out_specs=[pl.BlockSpec(memory_space=pltpu.VMEM)] * len(outs),
        scratch_shapes=list(scratch),
        cost_estimate=cost,
        compiler_params=grant(args, outs, scratch, room),
    )(*args)
    return result[0] if single else result


def plane_index():
    return lax.rem(lax.axis_index("dp"), plane_size())


def one_hot(rows, cols, offset):
    row = lax.broadcasted_iota(jnp.int32, (rows, cols), 0)
    col = lax.broadcasted_iota(jnp.int32, (rows, cols), 1)
    return (col == row + offset).astype(BF)


def three(row):
    hi = row.astype(BF)
    rest = row - hi.astype(F32)
    mid = rest.astype(BF)
    low = (rest - mid.astype(F32)).astype(BF)
    index = lax.broadcasted_iota(jnp.int32, (VEC, row.shape[1]), 0)
    zero = jnp.zeros((VEC, row.shape[1]), F32)
    picked = jnp.where(index == 0, hi.astype(F32), zero)
    picked = jnp.where(index == 1, mid.astype(F32), picked)
    return jnp.where(index == 2, low.astype(F32), picked)


def two(vectors):
    hi = vectors.astype(BF).astype(F32)
    return hi, vectors - hi


def rows_of(vectors, width):
    index = lax.broadcasted_iota(jnp.int32, (VEC, width), 0)
    out = jnp.zeros((VEC, width), F32)
    for i, v in enumerate(vectors):
        out = jnp.where(index == i, v, out)
    return out


def standardize(values):
    centred = values - jnp.mean(values, axis=-1, keepdims=True)
    rstd = lax.rsqrt(jnp.mean(centred * centred, axis=-1, keepdims=True) + NORM_EPS)
    return centred * rstd, rstd


def norm_backward(grad_normed, xhat, rstd, gain):
    scaled = grad_normed * gain
    inner = jnp.mean(scaled * xhat, axis=-1, keepdims=True)
    return rstd * (scaled - jnp.mean(scaled, axis=-1, keepdims=True) - xhat * inner)


def join(blocks):
    rows, cols = blocks[0].shape

    def body(*refs):
        for i, ref in enumerate(refs[:-1]):
            refs[-1][i * rows : (i + 1) * rows] = ref[...]

    return call(body, shape(rows * len(blocks), cols, blocks[0].dtype), blocks)


def prepare_rows(block_input, w_out):
    own, width = block_input.shape
    cols = w_out.shape[0]
    inner = cols // plane_size()

    def body(x_ref, w_ref, o_ref):
        part = dot(one_hot(inner, cols, plane_index() * inner), w_ref[...], 1, 0)
        o_ref[:own] = x_ref[...]
        o_ref[own:] = part.astype(BF)

    return call(body, shape(own + inner, width, BF), [block_input, w_out])


def prepare_weights(w_up, w_down, b_up):
    hidden, width = w_down.shape
    units = hidden // plane_size()
    padded = -(-units // 128) * 128

    def body(up_ref, down_ref, bias_ref, o_ref):
        offset = plane_index() * units
        pick = one_hot(units, hidden, offset)
        o_ref[:units] = dot(pick, up_ref[...], 1, 1).astype(BF)
        o_ref[units : 2 * units] = dot(pick, down_ref[...], 1, 0).astype(BF)
        row = lax.broadcasted_iota(jnp.int32, (padded, hidden), 0)
        wide = jnp.where(row < units, one_hot(padded, hidden, offset).astype(F32), 0.0).astype(BF)
        bias = dot(three(bias_ref[...]).astype(BF), wide, 1, 1)
        o_ref[2 * units :, :padded] = bias.astype(BF)
        o_ref[2 * units :, padded:] = jnp.zeros((VEC, width - padded), BF)

    return call(
        body, shape(2 * units + VEC, width, BF), [w_up, w_down, b_up[None]],
        flops=4 * units * hidden * width,
    )


def prepare_cotangent(lengths, cotangent):
    own, width = cotangent.shape

    def body(len_ref, cot_ref, out_ref):
        total = jnp.int32(0)
        for i in range(len_ref.shape[1]):
            total = total + len_ref[0, i]
        slot = lax.axis_index("tensor") * own + lax.broadcasted_iota(jnp.int32, (own, width), 0)
        cot = cot_ref[...].astype(F32)
        out_ref[...] = jnp.where(slot < total, cot, cot * 0.0).astype(BF)

    return call(body, shape(own, width, BF), [lengths, cotangent], smem=1)


def prepare_out(blocks, own, inner):
    width = blocks[0].shape[1]

    def body(*refs):
        parts = [ref[own : own + inner].astype(F32) for ref in refs[:-1]]
        refs[-1][...] = jnp.concatenate(parts, axis=0).astype(BF)

    return call(body, shape(len(blocks) * inner, width, BF), list(blocks))


def allowed_pairs(len_ref, own, nz):
    t = lax.axis_index("tensor")
    n = own * nz

    def slots(index):
        out = jnp.zeros(index.shape, jnp.int32)
        for m in range(nz):
            inside = (index >= m * own) & (index < (m + 1) * own)
            out = jnp.where(inside, index - m * own + (t ^ m) * own, out)
        return out

    query = slots(lax.broadcasted_iota(jnp.int32, (1, n), 1))
    key = slots(lax.broadcasted_iota(jnp.int32, (n, 1), 0))
    start = jnp.zeros((1, n), jnp.int32)
    end = jnp.int32(0)
    for i in range(len_ref.shape[1]):
        end = end + len_ref[0, i]
        start = jnp.where(query >= end, end, start)
    return (key <= query) & (key >= start)


def attention_forward(lengths, blocks, own, w_t, b_query, b_value, gain, bias):
    nz = len(blocks)
    n = own * nz
    width = w_t.shape[1]
    cols = w_t.shape[0]
    heads = cols // (3 * HD)

    def body(len_ref, *refs):
        xs, refs = refs[:nz], refs[nz:]
        w_ref, bq_ref, bv_ref, g_ref, b_ref = refs[:5]
        att_refs, (qkv_ref, rows_ref, log_ref) = refs[5 : 5 + nz], refs[5 + nz :]
        for m in range(nz):
            xhat, _ = standardize(xs[m][:own].astype(F32))
            rows_ref[m * own : (m + 1) * own] = (xhat * g_ref[...] + b_ref[...]).astype(BF)
        joined = dot(w_ref[...], rows_ref[...], 1, 1)
        ones = jnp.ones((VEC, n), BF)
        bias_q = dot(three(bq_ref[...]).astype(BF), ones, 0, 0)
        bias_v = dot(three(bv_ref[...]).astype(BF), ones, 0, 0)
        allowed = allowed_pairs(len_ref, own, nz)
        log_ref[...] = jnp.zeros(log_ref.shape, F32)
        for h in range(heads):
            base = h * 3 * HD
            q = (joined[base : base + HD] + bias_q[h * HD : (h + 1) * HD]).astype(BF)
            k = joined[base + HD : base + 2 * HD].astype(BF)
            v = (joined[base + 2 * HD : base + 3 * HD] + bias_v[h * HD : (h + 1) * HD]).astype(BF)
            qkv_ref[base : base + HD] = q
            qkv_ref[base + HD : base + 2 * HD] = k
            qkv_ref[base + 2 * HD : base + 3 * HD] = v
            scores = jnp.where(allowed, dot(k, q, 0, 0) * SCALE, -jnp.inf)
            top = jnp.max(scores, axis=0, keepdims=True)
            log_total = top + jnp.log(jnp.sum(jnp.exp(scores - top), axis=0, keepdims=True))
            log_ref[h : h + 1] = log_total
            probs = jnp.exp(scores - log_total).astype(BF)
            out = dot(v, probs, 1, 0).astype(BF)
            for m in range(nz):
                att_refs[m][h * HD : (h + 1) * HD] = out[:, m * own : (m + 1) * own]

    outs = [shape(heads * HD, own, BF)] * nz
    outs += [shape(cols, n, BF), shape(n, width, BF), shape(VEC, n, F32)]
    out = call(
        body, outs,
        [lengths, *blocks, w_t, b_query[None], b_value[None], gain[None], bias[None]],
        flops=2 * n * width * cols + 4 * heads * n * n * HD, smem=1, room=8 << 20,
    )
    return out[:nz], *out[nz:]


def place_out(mine, other, inner, nz):
    sub = plane_size()
    width = mine.shape[1]
    rows = mine.shape[0] // (sub // 2)
    cols = inner * sub

    def body(mine_ref, other_ref, o_ref, acc):
        p = plane_index()
        for core, ref in enumerate((mine_ref, other_ref)):
            for k in range(sub // 2):
                part = ref[k * rows : (k + 1) * rows].astype(F32)
                j = p ^ (2 * k + core)
                for m in range(nz):
                    at = pl.multiple_of(m * cols + j * inner, 8)
                    acc[pl.ds(at, inner)] = part[m * inner : (m + 1) * inner]
        o_ref[...] = acc[...].astype(BF)

    return call(
        body, shape(nz * cols, width, BF), [mine, other],
        scratch=[pltpu.VMEM((nz * cols, width), F32)],
    )


def middle(att, out_full, block_input, b_out, gain, bias):
    own, width = block_input.shape
    nz = len(att)

    def body(*refs):
        w_ref, x_ref, bo_ref, g_ref, b_ref, res_ref, n_ref = refs[nz:]
        cat = jnp.concatenate([r[...] for r in refs[:nz]], axis=0)
        res = x_ref[...].astype(F32) + dot(cat, w_ref[...], 0, 0) + bo_ref[...]
        res_ref[...] = res
        xhat, _ = standardize(res)
        n_ref[...] = (xhat * g_ref[...] + b_ref[...]).astype(BF)

    return call(
        body, [shape(own, width, F32), shape(own, width, BF)],
        [*att, out_full, block_input, b_out[None], gain[None], bias[None]],
        flops=2 * own * width * width,
    )


def grid_call(body, steps, args, specs, outs, out_specs, scratch, flops):
    cost = pl.CostEstimate(
        flops=flops,
        bytes_accessed=sum(size_of(a) for a in args) + sum(size_of(o) for o in outs),
        transcendentals=0,
    )
    return pl.pallas_call(
        body, grid=(steps,), in_specs=specs, out_specs=out_specs, out_shape=outs,
        scratch_shapes=scratch, cost_estimate=cost,
        compiler_params=grant(args, outs, scratch, 4 << 20),
    )(*args)


def stepped(rows, cols):
    return pl.BlockSpec((rows, cols), lambda i: (i, 0))


def fixed(rows, cols):
    return pl.BlockSpec((rows, cols), lambda i: (0, 0))


def feed_forward(mine, other, mine_cot, other_cot, weights, own):
    width = mine.shape[1]
    steps = mine.shape[0] // own
    nz = len(weights)
    units = (weights[0].shape[0] - VEC) // 2
    padded = -(-units // 128) * 128
    hidden = nz * units
    cot_rows = mine_cot.shape[0] // steps

    def body(*refs):
        x0, x1, c0, c1 = refs[:4]
        w_refs = refs[4 : 4 + nz]
        keep, send, act_ref, pre_ref, bg_ref, up, down, bias_ref = refs[4 + nz :]
        step = pl.program_id(0)

        @pl.when(step == 0)
        def _():
            total = jnp.zeros((VEC, hidden), F32)
            for m in range(nz):
                up[m * units : (m + 1) * units] = w_refs[m][:units]
                down[m * units : (m + 1) * units] = w_refs[m][units : 2 * units]
                place = one_hot(padded, hidden, m * units)
                total = total + dot(w_refs[m][2 * units :, :padded], place, 1, 0)
            bias_ref[...] = jnp.broadcast_to(jnp.sum(total, axis=0, keepdims=True), (VEC, hidden))
            bg_ref[...] = jnp.zeros(bg_ref.shape, F32)

        rows = jnp.concatenate([x0[...], x1[...]], axis=0)
        cot = jnp.concatenate([c0[:own], c1[:own]], axis=0)
        values = dot(rows, up[...], 1, 1) + bias_ref[0:1]
        squared = values * values
        tangent = jnp.tanh(GELU_COEF * (values + GELU_CUBE * squared * values))
        half = 0.5 * (1.0 + tangent)
        act_ref[...] = (values * half).astype(BF)
        slope = half + 0.5 * values * (1.0 - tangent * tangent) * GELU_COEF * (
            1.0 + 3.0 * GELU_CUBE * squared
        )
        grad = dot(cot, down[...], 1, 1) * slope
        bg_ref[...] += jnp.broadcast_to(jnp.sum(grad, axis=0, keepdims=True), (VEC, hidden))
        grad = grad.astype(BF)
        pre_ref[...] = grad
        back = dot(grad, up[...], 1, 0)
        keep[...] = back[:own]
        send[...] = back[own:].astype(BF)

    n = 2 * steps * own
    return grid_call(
        body, steps, [mine, other, mine_cot, other_cot, *weights],
        [stepped(own, width)] * 2 + [stepped(cot_rows, width)] * 2
        + [fixed(*weights[0].shape)] * nz,
        [shape(n // 2, width, F32), shape(n // 2, width, BF), shape(n, hidden, BF),
         shape(n, hidden, BF), shape(VEC, hidden, F32)],
        [stepped(own, width)] * 2 + [stepped(2 * own, hidden)] * 2 + [fixed(VEC, hidden)],
        [pltpu.VMEM((hidden, width), BF), pltpu.VMEM((hidden, width), BF),
         pltpu.VMEM((VEC, hidden), F32)],
        6 * n * hidden * width,
    )


def feed_forward_weights(mine, other, mine_cot, other_cot, weights, act, pre, bias_grad, own):
    width = mine.shape[1]
    steps = mine.shape[0] // own
    nz = len(weights)
    units = (weights[0].shape[0] - VEC) // 2
    padded = -(-units // 128) * 128
    hidden = nz * units
    cot_rows = mine_cot.shape[0] // steps

    def body(*refs):
        x0, x1, c0, c1, act_ref, pre_ref, bg_ref = refs[:7]
        w_refs = refs[7 : 7 + nz]
        keep, send = refs[7 + nz : 9 + nz]
        packs = refs[9 + nz : 9 + 2 * nz]
        up_sum, down_sum, down = refs[9 + 2 * nz :]
        step = pl.program_id(0)

        @pl.when(step == 0)
        def _():
            for m in range(nz):
                down[m * units : (m + 1) * units] = w_refs[m][units : 2 * units]
            up_sum[...] = jnp.zeros(up_sum.shape, F32)
            down_sum[...] = jnp.zeros(down_sum.shape, F32)

        rows = jnp.concatenate([x0[...], x1[...]], axis=0)
        cot = jnp.concatenate([c0[:own], c1[:own]], axis=0)
        up_sum[...] += dot(pre_ref[...], rows, 0, 0)
        down_sum[...] += dot(act_ref[...], cot, 0, 0)
        out = dot(act_ref[...], down[...], 1, 0)
        keep[...] = out[:own]
        send[...] = out[own:].astype(BF)

        @pl.when(step == steps - 1)
        def _():
            bias_rows = three(bg_ref[0:1]).astype(BF)
            for m in range(nz):
                kind = packs[m].dtype
                part = slice(m * units, (m + 1) * units)
                packs[m][:units] = up_sum[part].astype(kind)
                packs[m][units : 2 * units] = down_sum[part].astype(kind)
                row = lax.broadcasted_iota(jnp.int32, (padded, hidden), 0)
                place = one_hot(padded, hidden, m * units).astype(F32)
                place = jnp.where(row < units, place, 0.0).astype(BF)
                packs[m][2 * units :, :padded] = dot(bias_rows, place, 1, 1).astype(kind)
                packs[m][2 * units :, padded:] = jnp.zeros((VEC, width - padded), kind)

    n = 2 * steps * own
    outs = [shape(n // 2, width, F32), shape(n // 2, width, BF)]
    outs += [shape(2 * units + VEC, width, F32 if m == 0 else BF) for m in range(nz)]
    out = grid_call(
        body, steps, [mine, other, mine_cot, other_cot, act, pre, bias_grad, *weights],
        [stepped(own, width)] * 2 + [stepped(cot_rows, width)] * 2
        + [stepped(2 * own, hidden)] * 2 + [fixed(VEC, hidden)] + [fixed(*weights[0].shape)] * nz,
        outs,
        [stepped(own, width)] * 2 + [fixed(2 * units + VEC, width)] * nz,
        [pltpu.VMEM((hidden, width), F32), pltpu.VMEM((hidden, width), F32),
         pltpu.VMEM((hidden, width), BF)],
        6 * n * hidden * width,
    )
    return out[0], out[1], out[2:]


def fold(keep, got, vec_at=None):
    blocks = plane_size() // 2
    rows = keep.shape[0] // blocks
    width = keep.shape[1]

    def body(keep_ref, got_ref, *outs):
        for k in range(blocks):
            part = slice(k * rows, (k + 1) * rows)
            total = keep_ref[part] + got_ref[part].astype(F32)
            if vec_at is not None:
                hi, low = two(total[vec_at : vec_at + VEC] + total[vec_at + VEC : vec_at + 2 * VEC])
                pieces = [total[:vec_at], hi, low]
                if vec_at + 2 * VEC < rows:
                    pieces.append(total[vec_at + 2 * VEC :])
                total = jnp.concatenate(pieces, axis=0)
            outs[k][...] = total.astype(outs[k].dtype)

    outs = [shape(rows, width, F32 if k == 0 else BF) for k in range(blocks)]
    return call(body, outs, [keep, got])


def total_of(refs):
    total = refs[0][...].astype(F32)
    for ref in refs[1:]:
        total = total + ref[...].astype(F32)
    return total


def second_backward(parts, residual, cot_rows, gain, out_full, nz):
    own, width = residual.shape
    cols = out_full.shape[0] // nz
    count = len(parts)

    def body(*refs):
        res_ref, cot_ref, g_ref, w_ref = refs[count : count + 4]
        grad_ref, bf_ref, vec_ref = refs[count + 4 : count + 7]
        outs = refs[count + 7 :]
        grad = total_of(refs[:count])
        xhat, rstd = standardize(res_ref[...])
        cot = cot_ref[...].astype(F32)
        grad_res = cot + norm_backward(grad, xhat, rstd, g_ref[...])
        grad_ref[...] = grad_res
        low = grad_res.astype(BF)
        bf_ref[...] = low
        for m in range(nz):
            outs[m][...] = dot(w_ref[m * cols : (m + 1) * cols], low, 1, 1).astype(BF)
        sums = [jnp.sum(v, axis=0, keepdims=True) for v in (cot, grad * xhat, grad, grad_res)]
        vec_ref[...] = rows_of(sums, width)

    out = call(
        body,
        [shape(own, width, F32), shape(own, width, BF), shape(VEC, width, F32)]
        + [shape(cols, own, BF)] * nz,
        [*parts, residual, cot_rows, gain[None], out_full],
        flops=2 * own * width * width,
    )
    return out[0], out[1], out[2], out[3:]


def out_gradient(att, grad_res_bf, mlp_keep, mlp_send, vec):
    sub, nz = plane_size(), len(att)
    cols, own = att[0].shape
    width = vec.shape[1]
    inner = cols // sub
    grad_rows = nz * inner
    rows = grad_rows + own + 2 * VEC
    blocks = sub // 2

    def body(*refs):
        g_ref, keep_in, send_in, vec_ref, keep, send, acc = refs[nz:]
        for m in range(nz):
            acc[m * cols : (m + 1) * cols] = dot(refs[m][...], g_ref[...], 1, 0)
        p = plane_index()
        hi, low = two(vec_ref[...])
        for core, ref in enumerate((keep, send)):
            for k in range(blocks):
                j = p ^ (2 * k + core)
                part = jnp.concatenate(
                    [
                        acc[pl.ds(pl.multiple_of(m * cols + j * inner, 8), inner)]
                        for m in range(nz)
                    ],
                    axis=0,
                )
                at = k * rows
                ref[at : at + grad_rows] = part.astype(ref.dtype)
                source = keep_in if core == 0 else send_in
                ref[at + grad_rows : at + grad_rows + own] = source[k * own : (k + 1) * own]
                ref[at + grad_rows + own : at + rows] = jnp.concatenate([hi, low], axis=0).astype(
                    ref.dtype
                )

    return call(
        body, [shape(blocks * rows, width, F32), shape(blocks * rows, width, BF)],
        [*att, grad_res_bf, mlp_keep, mlp_send, vec],
        flops=2 * own * width * width,
        scratch=[pltpu.VMEM((nz * cols, width), F32)],
    )


def block_result(parts, residual, b_down, late, lengths, nz):
    own, width = residual.shape
    count = len(parts)
    grad_rows = parts[0].shape[0] - own - 2 * VEC
    inner = grad_rows // nz

    def body(len_ref, *refs):
        res_ref, b_ref, late_ref, out_ref = refs[count : count + 4]
        packs = refs[count + 4 :]
        total = total_of(refs[:count])
        length = jnp.int32(0)
        for i in range(len_ref.shape[1]):
            length = length + len_ref[0, i]
        slot = lax.axis_index("tensor") * own + lax.broadcasted_iota(jnp.int32, (own, width), 0)
        final = res_ref[...] + total[grad_rows : grad_rows + own] + b_ref[...]
        out_ref[...] = jnp.where(slot < length, final, final * 0.0).astype(BF)
        at = grad_rows + own
        vec = total[at : at + VEC] + total[at + VEC : at + 2 * VEC]
        index = lax.broadcasted_iota(jnp.int32, (VEC, width), 0)
        for i in range(2):
            vec = jnp.where(index == 4 + i, late_ref[i : i + 1], vec)
        hi, low = two(vec)
        for m in range(nz):
            pack = jnp.concatenate([total[m * inner : (m + 1) * inner], hi, low], axis=0)
            packs[m][...] = pack.astype(packs[m].dtype)

    outs = [shape(own, width, BF)]
    outs += [shape(inner + 2 * VEC, width, F32 if m == 0 else BF) for m in range(nz)]
    out = call(body, outs, [lengths, *parts, residual, b_down[None], late], smem=1)
    return out[0], out[1:]


def weight_sums(ffn, out):
    count = len(ffn)
    rows, width = ffn[0].shape
    inner = out[0].shape[0] - 2 * VEC

    def body(*refs):
        pack_ref, vec_ref = refs[2 * count :]
        total = total_of(refs[:count])
        bias = jnp.sum(total[rows - VEC :], axis=0, keepdims=True)
        other = total_of(refs[count : 2 * count])
        vec_ref[...] = other[inner : inner + VEC] + other[inner + VEC :]
        pack_ref[...] = jnp.concatenate(
            [total[: rows - VEC], three(bias), other[:inner]], axis=0
        ).astype(BF)

    return call(body, [shape(rows + inner, width, BF), shape(VEC, width, F32)], [*ffn, *out])


def attention_backward(lengths, qkv, logs, att, grad_att, blocks, w_t, own):
    nz = len(blocks)
    cols, n = qkv.shape
    width = w_t.shape[1]
    heads = cols // (3 * HD)

    def body(len_ref, *refs):
        qkv_ref, log_ref = refs[:2]
        att_refs, ga_refs, xs = (refs[2 + i * nz : 2 + (i + 1) * nz] for i in range(3))
        w_ref = refs[2 + 3 * nz]
        outs = refs[3 + 3 * nz : 3 + 4 * nz]
        joined_ref, vec_ref, delta_rows = refs[3 + 4 * nz :]
        allowed = allowed_pairs(len_ref, own, nz)
        ga_all = jnp.concatenate([r[...] for r in ga_refs], axis=1)
        att_all = jnp.concatenate([r[...] for r in att_refs], axis=1)
        prod = ga_all.astype(F32) * att_all.astype(F32)
        for h in range(heads):
            base = h * 3 * HD
            q, k, v = (qkv_ref[base + i * HD : base + (i + 1) * HD] for i in range(3))
            ga = ga_all[h * HD : (h + 1) * HD]
            scores = jnp.where(allowed, dot(k, q, 0, 0) * SCALE, -jnp.inf)
            probs = jnp.exp(scores - log_ref[h : h + 1])
            grad_v = dot(ga, probs.astype(BF), 1, 1)
            delta = jnp.sum(prod[h * HD : (h + 1) * HD], axis=0, keepdims=True)
            grad_s = (probs * (dot(v, ga, 0, 0) - delta) * SCALE).astype(BF)
            grad_q = dot(k, grad_s, 1, 0)
            grad_k = dot(q, grad_s, 1, 1)
            joined_ref[base : base + HD] = grad_q.astype(BF)
            joined_ref[base + HD : base + 2 * HD] = grad_k.astype(BF)
            joined_ref[base + 2 * HD : base + 3 * HD] = grad_v.astype(BF)
            delta_rows[h * HD : (h + 1) * HD] = grad_q
            delta_rows[(heads + h) * HD : (heads + h + 1) * HD] = grad_v
        biases = lax.dot_general(
            jnp.ones((VEC, n), F32), delta_rows[...], (((1,), (1,)), ((), ())),
            precision=lax.Precision.HIGHEST, preferred_element_type=F32,
        )
        gain_sum = jnp.zeros((1, width), F32)
        bias_sum = jnp.zeros((1, width), F32)
        for m in range(nz):
            part = dot(joined_ref[:, m * own : (m + 1) * own], w_ref[...], 0, 0)
            outs[m][...] = part.astype(outs[m].dtype)
            xhat, _ = standardize(xs[m][:own].astype(F32))
            gain_sum = gain_sum + jnp.sum(part * xhat, axis=0, keepdims=True)
            bias_sum = bias_sum + jnp.sum(part, axis=0, keepdims=True)
        vec_ref[...] = rows_of([gain_sum, bias_sum], width)
        vec_ref[2:3, : 2 * heads * HD] = biases[0:1]

    outs = [shape(own, width, F32 if m == 0 else BF) for m in range(nz)]
    outs += [shape(cols, n, BF), shape(VEC, width, F32)]
    out = call(
        body, outs, [lengths, qkv, logs, *att, *grad_att, *blocks, w_t], smem=1,
        flops=2 * n * width * cols + 10 * heads * n * n * HD,
        scratch=[pltpu.VMEM((2 * heads * HD, n), F32)], room=12 << 20,
    )
    return out[:nz], out[nz], out[nz + 1]


def joined_gradient(joined, rows_one, vec):
    cols, n = joined.shape
    width = rows_one.shape[1]
    sub = plane_size()
    inner = cols // sub
    blocks = sub // 2
    rows = -(-(inner + 2 * VEC) // 16) * 16
    rest = rows - inner - 2 * VEC

    def body(g_ref, x_ref, vec_ref, keep, send, acc):
        acc[...] = dot(g_ref[...], x_ref[...], 1, 0)
        p = plane_index()
        hi, low = two(vec_ref[...])
        tail = [hi, low] + ([jnp.zeros((rest, width), F32)] if rest else [])
        for core, ref in enumerate((keep, send)):
            for k in range(blocks):
                j = p ^ (2 * k + core)
                part = acc[pl.ds(pl.multiple_of(j * inner, 8), inner)]
                ref[k * rows : (k + 1) * rows] = jnp.concatenate([part, *tail], axis=0).astype(
                    ref.dtype
                )

    return call(
        body, [shape(blocks * rows, width, F32), shape(blocks * rows, width, BF)],
        [joined, rows_one, vec], flops=2 * cols * n * width,
        scratch=[pltpu.VMEM((cols, width), F32)],
    )


def joined_sums(parts, inner):
    width = parts[0].shape[1]
    count = len(parts)

    def body(*refs):
        total = total_of(refs[:count])
        refs[count][...] = total[:inner].astype(BF)
        refs[count + 1][...] = total[inner : inner + VEC] + total[inner + VEC : inner + 2 * VEC]

    return call(body, [shape(inner, width, BF), shape(VEC, width, F32)], list(parts))


def first_backward(parts, block_input, grad_res, gain):
    own, width = grad_res.shape
    count = len(parts)

    def body(*refs):
        x_ref, r_ref, g_ref, out_ref = refs[count:]
        grad = total_of(refs[:count])
        xhat, rstd = standardize(x_ref[...].astype(F32))
        out_ref[...] = r_ref[...] + norm_backward(grad, xhat, rstd, g_ref[...])

    return call(body, shape(own, width, F32), [*parts, block_input, grad_res, gain[None]])


def assemble_weights(mine, other, units, inner):
    sub = plane_size()
    width = mine.shape[1]
    rows = mine.shape[0] // (sub // 2)
    hidden, cols = sub * units, sub * inner
    padded = -(-units // 128) * 128

    def body(mine_ref, other_ref, up_ref, down_ref, bias_ref, out_ref, acc):
        p = plane_index()
        bias = jnp.zeros((VEC, hidden), F32)
        for core, ref in enumerate((mine_ref, other_ref)):
            for k in range(sub // 2):
                j = p ^ (2 * k + core)
                at = pl.multiple_of(j * units, 8)
                part = ref[k * rows : (k + 1) * rows].astype(F32)
                acc[pl.ds(at, units)] = part[:units]
                down_ref[pl.ds(at, units)] = part[units : 2 * units]
                place = one_hot(padded, hidden, at)
                row = lax.broadcasted_iota(jnp.int32, (padded, hidden), 0)
                place = jnp.where(row < units, place.astype(F32), 0.0).astype(BF)
                tail = part[2 * units : 2 * units + VEC, :padded].astype(BF)
                bias = bias + dot(tail, place, 1, 0)
                out_ref[pl.ds(pl.multiple_of(j * inner, 8), inner)] = part[2 * units + VEC :]
        bias_ref[...] = jnp.broadcast_to(jnp.sum(bias, axis=0, keepdims=True), (VEC, hidden))
        up_ref[...] = jnp.transpose(acc[...])

    return call(
        body,
        [shape(width, hidden, F32), shape(hidden, width, F32), shape(VEC, hidden, F32),
         shape(cols, width, F32)],
        [mine, other], scratch=[pltpu.VMEM((hidden, width), F32)],
    )


def assemble_joined(mine, other):
    sub = plane_size()
    width = mine.shape[1]
    inner = mine.shape[0] // (sub // 2)

    def body(mine_ref, other_ref, out_ref):
        p = plane_index()
        for core, ref in enumerate((mine_ref, other_ref)):
            whole = ref[...].astype(F32)
            for k in range(sub // 2):
                j = p ^ (2 * k + core)
                out_ref[pl.ds(pl.multiple_of(j * inner, 8), inner)] = whole[
                    k * inner : (k + 1) * inner
                ]

    return call(body, shape(sub * inner, width, F32), [mine, other])


def local(
    block_input,
    seq_lengths,
    w_qkv,
    b_query,
    b_value,
    w_out,
    b_out,
    w_up,
    b_up,
    w_down,
    b_down,
    first_norm_gain,
    first_norm_bias,
    second_norm_gain,
    second_norm_bias,
    cotangent,
):
    own, _ = block_input.shape
    nz, sub = z_size(), plane_size()
    cols = w_out.shape[0]
    inner = cols // sub
    units = w_down.shape[0] // sub
    w_t = w_qkv.T

    row_pack = prepare_rows(block_input, w_out)
    row_blocks = [row_pack] + gather_z(row_pack)
    cot = prepare_cotangent(seq_lengths, cotangent)
    cot_mine, cot_other = gather_plane(cot)
    weight_pack = prepare_weights(w_up, w_down, b_up)
    out_mine, out_other = gather_plane(prepare_out(row_blocks, own, inner))

    att_sent, qkv, rows_one, logs = attention_forward(
        seq_lengths, row_blocks, own, w_t, b_query, b_value, first_norm_gain, first_norm_bias
    )
    att = [att_sent[0]] + send_z(att_sent[1:])
    weights = [weight_pack] + gather_z(weight_pack)
    out_full = place_out(out_mine, out_other, inner, nz)
    residual, normed_two = middle(
        att, out_full, block_input, b_out, second_norm_gain, second_norm_bias
    )
    mine, other = gather_plane(normed_two)

    keep, send, act, pre, bias_grad = feed_forward(
        mine, other, cot_mine, cot_other, weights, own
    )
    got = swap(send, "dp", 1)
    mlp_keep, mlp_send, ffn_packs = feed_forward_weights(
        mine, other, cot_mine, cot_other, weights, act, pre, bias_grad, own
    )
    folded = fold(keep, got)
    grad_res, grad_res_bf, early, grad_att_sent = second_backward(
        [folded[0]] + send_plane(folded[1:]), residual, cot, second_norm_gain, out_full, nz
    )
    grad_att = [grad_att_sent[0]] + send_z(grad_att_sent[1:])

    first_parts, joined, late = attention_backward(
        seq_lengths, qkv, logs, att_sent, grad_att, row_blocks, w_t, own
    )
    first_got = send_z(first_parts[1:])
    grad_input = first_backward(
        [first_parts[0]] + first_got, block_input, grad_res, first_norm_gain
    )

    joined_keep, joined_send = joined_gradient(joined, rows_one, late)
    joined_inner = joined.shape[0] // sub
    joined_folded = fold(joined_keep, swap(joined_send, "dp", 1), joined_inner)
    joined_sum, late_sum = joined_sums(
        [joined_folded[0]] + send_plane(joined_folded[1:]), joined_inner
    )
    grad_w_qkv = assemble_joined(*gather_plane(beyond(joined_sum).astype(BF))).T
    bias_sum = beyond(late_sum)[2]

    ffn_got = send_z(ffn_packs[1:])
    out_keep, out_send = out_gradient(att, grad_res_bf, mlp_keep, mlp_send, early)
    out_folded = fold(out_keep, swap(out_send, "dp", 1), nz * inner + own)
    block_output, out_packs = block_result(
        [out_folded[0]] + send_plane(out_folded[1:]), residual, b_down, late_sum, seq_lengths, nz
    )
    out_got = send_z(out_packs[1:])
    weight_pack_sum, early_sum = weight_sums(
        [beyond(x) for x in [ffn_packs[0], *ffn_got]], [beyond(x) for x in [out_packs[0], *out_got]]
    )
    grad_w_up, grad_w_down, grad_b_up, grad_w_out = assemble_weights(
        *gather_plane(weight_pack_sum), units, inner
    )

    return (
        block_output,
        grad_input,
        grad_w_qkv,
        bias_sum[:cols],
        bias_sum[cols : 2 * cols],
        grad_w_out,
        early_sum[3],
        grad_w_up,
        grad_b_up[0],
        grad_w_down,
        early_sum[0],
        early_sum[4],
        early_sum[5],
        early_sum[1],
        early_sum[2],
    )


def solution(mesh):
    rows, cols = P(("dp", "tensor"), None), P(None, "tensor")
    vec, tall, full = P("tensor"), P("tensor", None), P()
    placed = (
        rows, P("dp", None), cols, vec, vec, tall, full, cols, vec, tall,
        full, full, full, full, full, rows,
    )
    given = (
        rows, rows, cols, vec, vec, tall, full, cols, vec, tall,
        full, full, full, full, full,
    )

    return jax.shard_map(local, mesh=mesh, in_specs=placed, out_specs=given, check_vma=False)
```

time: 382 us -> 237 us (0.62)
  blocking collectives: 138 us -> 0 us
  starting transfers between devices: 0.21 us -> 69 us
  waiting for transfers between devices: 168 us -> 133 us
  matrix products: 30 us -> 0 us
  Pallas kernels: 0 us -> 28.9 us
  other arithmetic: 14.4 us -> 0 us
  between operations: 14.2 us -> 1.13 us
  local copies, waits for them, and re-layouts: 15.9 us -> 3.88 us
    ppermute x0 -> x53, waiting for transfers between devices: none -> 133 us  [swap(): return lax.ppermute(x, axis, [(i, i ^ mask) for i in range(n)])]
    reduce_scatter x4 -> x0, waiting for transfers between devices: 94.2 us -> none  [the longest x1 36 us: local(): lax.psum_scatter(jnp.dot(activation, w_down, preferred_element_type=jnp.f...]
    all_gather x4 -> x0, blocking collectives: 84.9 us -> none  [the longest x1 26.8 us: local(): final_all = lax.all_gather(grad_final_bf, 'tensor', axis=0, tiled=True)]
    psum x1 -> x0, waiting for transfers between devices: 73.4 us -> none  [local(): lax.psum((grad_w_qkv, grad_b_query, grad_b_value, grad_w_out, grad_w_up,...]
    ppermute x0 -> x53, starting transfers between devices: none -> 69 us  [swap(): return lax.ppermute(x, axis, [(i, i ^ mask) for i in range(n)])]
    psum x2 -> x0, blocking collectives: 53.6 us -> none  [the longest x1 40.5 us: local(): lax.psum((first_norm_gain_gradient, first_norm_bias_gradient, second_norm...]
    dot_general x18 -> x0, matrix products: 30 us -> none  [the longest x4 9.05 us: contract_rows(): lax.dot_general(left, right, (((0,), (0,)), ((), ())), preferred_element_...]
    pallas_call x0 -> x27, Pallas kernels: none -> 28.9 us  [the longest x25 21.4 us: call(): pl.pallas_call(body, out_shape=outs, in_specs=given, out_specs=[pl.BlockS...]
  transfers between devices with their start and end apart: 5 -> 53, of which waited for: 5 -> 28; matrix products, arithmetic and copies ran while one was open for 5% -> 1% of each run, Pallas kernels for 0% -> 8%
where the time goes in v1:
time: 237 us; the launch traced here: 236 us
  waiting for transfers between devices  133 us (56%)
  starting transfers between devices  69 us (29%)
  Pallas kernels  28.9 us (12%)
  local copies, waits for them, and re-layouts  3.88 us (2%)
    ppermute x53, waiting for transfers between devices, swap(): return lax.ppermute(x, axis, [(i, i ^ mask) for i in range(n)])  133 us
    ppermute x53, starting transfers between devices, swap(): return lax.ppermute(x, axis, [(i, i ^ mask) for i in range(n)])  69 us
    pallas_call x25, Pallas kernels, call(): pl.pallas_call(body, out_shape=outs, in_specs=given, out_specs=[pl.BlockS...  21.4 us
    pallas_call x2, Pallas kernels, grid_call(): pl.pallas_call(body, grid=(steps,), in_specs=specs, out_specs=out_specs,...  7.46 us
  transfers between devices with their start and end apart: 53, of which 28 were waited for; matrix products, arithmetic and copies ran while one was open for 1% of the time, Pallas kernels for 8%

profile of v1, /device:TPU:0, one launch (start us, length us, event | category | flops | bytes accessed | tf_op | source)
XLA Modules:
  0.0 235.7 jit_solution(8983488281910405535)
XLA Ops:
  2.8 3.1 %collective-permute-start = (bf16[152,768]{1,0:T(8,128)(2,1)S(1)}, bf16[152,768]{1,0:T(8,128)(2,1)S(1)}, u32[]{:S(2)}, u32[]{:S(2)}) collective-permute-start(bf16[152,768]{1,0:T(8,128)(2,1)S(1)} %shard_map.271.refs_0_.refs_10_), channel_id=1, source_target_pairs={{0,1},{1,0},{2,3},{3,2},{4,5},{5,4},{6,7},{7,6},{8,9},{9,8},{10,11... | collective-permute-start | bytes 700424 | tf_op jit(solution)/shard_map/ppermute | solution.py:29
  8.5 7.4 %collective-permute-done.refs_1_.refs_11_ = bf16[152,768]{1,0:T(8,128)(2,1)S(1)} collective-permute-done((bf16[152,768]{1,0:T(8,128)(2,1)S(1)}, bf16[152,768]{1,0:T(8,128)(2,1)S(1)}, u32[]{:S(2)}, u32[]{:S(2)}) %collective-permute-start) | collective-permute-done | bytes 233504 | tf_op jit(solution)/shard_map/ppermute | solution.py:29
  15.8 9.5 %collective-permute-done.1.refs_2_.refs_12_ = bf16[152,768]{1,0:T(8,128)(2,1)S(1)} collective-permute-done((bf16[152,768]{1,0:T(8,128)(2,1)S(1)}, bf16[152,768]{1,0:T(8,128)(2,1)S(1)}, u32[]{:S(2)}, u32[]{:S(2)}) %collective-permute-start.1) | collective-permute-done | bytes 233504 | tf_op jit(solution)/shard_map/ppermute | solution.py:29
  35.9 3.7 %shard_map.272 = (bf16[192,128]{1,0:T(8,128)(2,1)S(1)}, bf16[192,128]{1,0:T(8,128)(2,1)S(1)}, bf16[192,128]{1,0:T(8,128)(2,1)S(1)}, bf16[192,128]{1,0:T(8,128)(2...) custom-call(s32[1,4]{1,0:T(1,128)S(1)} %copy-done.6, ...), custom_call_target="tpu_custom_call" | custom-call | flops 654311424 | bytes 3415568 | tf_op jit(solution)/shard_map/pallas_call | solution.py:90
  39.6 4.8 %collective-permute-start.3 = (bf16[192,128]{1,0:T(8,128)(2,1)S(1)}, bf16[192,128]{1,0:T(8,128)(2,1)S(1)}, u32[]{:S(2)}, u32[]{:S(2)}) collective-permute-start(bf16[192,128]{1,0:T(8,128)(2,1)S(1)} %get-tuple-element.78.refs_3_), channel_id=1, source_target_pairs={{0,1},{1,0},{2,3},{3,2},{4,5},{5,4},{6,7},{7,6},{8,9},{9,8},{10,11... | collective-permute-start | bytes 147464 | tf_op jit(solution)/shard_map/ppermute | solution.py:29
  55.7 4.3 %collective-permute-done.15.refs_2_ = bf16[128,768]{1,0:T(8,128)(2,1)S(1)} collective-permute-done((bf16[128,768]{1,0:T(8,128)(2,1)S(1)}, bf16[128,768]{1,0:T(8,128)(2,1)S(1)}, u32[]{:S(2)}, u32[]{:S(2)}) %collective-permute-start.15) | collective-permute-done | bytes 196640 | tf_op jit(solution)/shard_map/ppermute | solution.py:29
  60.8 5.3 %collective-permute-done.11.refs_2_ = bf16[128,768]{1,0:T(8,128)(2,1)S(1)} collective-permute-done((bf16[128,768]{1,0:T(8,128)(2,1)S(1)}, bf16[128,768]{1,0:T(8,128)(2,1)S(1)}, u32[]{:S(2)}, u32[]{:S(2)}) %collective-permute-start.11) | collective-permute-done | bytes 196640 | tf_op jit(solution)/shard_map/ppermute | solution.py:29
  71.4 11.4 %collective-permute-done.18.refs_5_.refs_8_ = bf16[200,768]{1,0:T(8,128)(2,1)S(1)} collective-permute-done((bf16[200,768]{1,0:T(8,128)(2,1)S(1)}, bf16[200,768]{1,0:T(8,128)(2,1)S(1)}, u32[]{:S(2)}, u32[]{:S(2)}) %collective-permute-start.18) | collective-permute-done | bytes 307232 | tf_op jit(solution)/shard_map/ppermute | solution.py:29
  82.8 9.2 %collective-permute-done.19.refs_6_.refs_9_ = bf16[200,768]{1,0:T(8,128)(2,1)S(1)} collective-permute-done((bf16[200,768]{1,0:T(8,128)(2,1)S(1)}, bf16[200,768]{1,0:T(8,128)(2,1)S(1)}, u32[]{:S(2)}, u32[]{:S(2)}) %collective-permute-start.19) | collective-permute-done | bytes 307232 | tf_op jit(solution)/shard_map/ppermute | solution.py:29
  92.0 3.9 %shard_map.281 = (f32[512,768]{1,0:T(8,128)S(1)}, bf16[512,768]{1,0:T(8,128)(2,1)S(1)}, bf16[1024,384]{1,0:T(8,128)(2,1)S(1)}, bf16[1024,384]{1,0:T(8,128)(2,1)S(1)}, f32[8,384]{1,0:T(8,128)S(1)}) custom-call(bf16[512,768]{1,0:T(8,128)(2,1)S(1)} %shard_map.277.refs_0_, bf16[512,768]{1,0:T(8,128)(2,1)S(1)} %collective-permute-done.13.refs_1_, ...), custom_call_target="tpu_custom_call" | custom-call | flops 1811939328 | bytes 8318976 | tf_op jit(solution)/shard_map/pallas_call | solution.py:334
  102.0 3.6 %shard_map.284 = (f32[512,768]{1,0:T(8,128)S(1)}, bf16[512,768]{1,0:T(8,128)(2,1)S(1)}, f32[200,768]{1,0:T(8,128)S(1)}, bf16[200,768]{1,0:T(8,128)(2,1)S(1)}, bf...) custom-call(bf16[512,768]{1,0:T(8,128)(2,1)S(1)} %shard_map.277.refs_0_, ...), custom_call_target="tpu_custom_call" | custom-call | flops 1811939328 | bytes 9854976 | tf_op jit(solution)/shard_map/pallas_call | solution.py:334
  106.3 4.7 %collective-permute-done.23.refs_2_ = bf16[128,768]{1,0:T(8,128)(2,1)S(1)} collective-permute-done((bf16[128,768]{1,0:T(8,128)(2,1)S(1)}, bf16[128,768]{1,0:T(8,128)(2,1)S(1)}, u32[]{:S(2)}, u32[]{:S(2)}) %collective-permute-start.23) | collective-permute-done | bytes 196640 | tf_op jit(solution)/shard_map/ppermute | solution.py:29
  112.6 6.4 %collective-permute-start.29 = (bf16[192,128]{1,0:T(8,128)(2,1)S(1)}, bf16[192,128]{1,0:T(8,128)(2,1)S(1)}, u32[]{:S(2)}, u32[]{:S(2)}) collective-permute-start(bf16[192,128]{1,0:T(8,128)(2,1)S(1)} %get-tuple-element.105), channel_id=1, source_target_pairs={{0,1},{1,0},{2,3},{3,2},{4,5},{5,4},{6,7},{7,6},{8,9},{9,8},{10,11... | collective-permute-start | bytes 147464 | tf_op jit(solution)/shard_map/ppermute | solution.py:29
  121.5 4.7 %collective-permute-done.30.refs_8_ = bf16[192,128]{1,0:T(8,128)(2,1)S(1)} collective-permute-done((bf16[192,128]{1,0:T(8,128)(2,1)S(1)}, bf16[192,128]{1,0:T(8,128)(2,1)S(1)}, u32[]{:S(2)}, u32[]{:S(2)}) %collective-permute-start.30) | collective-permute-done | bytes 49184 | tf_op jit(solution)/shard_map/ppermute | solution.py:29
  126.2 4.7 %shard_map.287 = (f32[128,768]{1,0:T(8,128)S(1)}, bf16[128,768]{1,0:T(8,128)(2,1)S(1)}, bf16[128,768]{1,0:T(8,128)(2,1)S(1)}, bf16[128,768]{1,0:T(8,128)(2,1)S(1...) custom-call(s32[1,4]{1,0:T(1,128)S(1)} %copy-done.6, bf16[576,512]{1,0:T(8,128)(2,1)S(1)} %get-tuple-element.102.refs_0_, ...), custom_call_target="tpu_custom_call" | custom-call | flops 956301312 | bytes 4415504 | tf_op jit(solution)/shard_map/pallas_call | solution.py:90
  138.5 8.3 %collective-permute-done.33.refs_1_ = bf16[96,768]{1,0:T(8,128)(2,1)S(1)} collective-permute-done((bf16[96,768]{1,0:T(8,128)(2,1)S(1)}, bf16[96,768]{1,0:T(8,128)(2,1)S(1)}, u32[]{:S(2)}, u32[]{:S(2)}) %collective-permute-start.33) | collective-permute-done | bytes 147488 | tf_op jit(solution)/shard_map/ppermute | solution.py:29
  154.3 5.0 %collective-permute-done.27.refs_2_ = bf16[240,768]{1,0:T(8,128)(2,1)S(1)} collective-permute-done((bf16[240,768]{1,0:T(8,128)(2,1)S(1)}, bf16[240,768]{1,0:T(8,128)(2,1)S(1)}, u32[]{:S(2)}, u32[]{:S(2)}) %collective-permute-start.27) | collective-permute-done | bytes 368672 | tf_op jit(solution)/shard_map/ppermute | solution.py:29
  165.0 12.3 %collective-permute-done.44.refs_2_ = bf16[200,768]{1,0:T(8,128)(2,1)S(1)} collective-permute-done((bf16[200,768]{1,0:T(8,128)(2,1)S(1)}, bf16[200,768]{1,0:T(8,128)(2,1)S(1)}, u32[]{:S(2)}, u32[]{:S(2)}) %collective-permute-start.44) | collective-permute-done | bytes 307232 | tf_op jit(solution)/shard_map/ppermute | solution.py:29
  177.4 6.7 %collective-permute-done.47.refs_6_ = bf16[40,768]{1,0:T(8,128)(2,1)S(1)} collective-permute-done((bf16[40,768]{1,0:T(8,128)(2,1)S(1)}, bf16[40,768]{1,0:T(8,128)(2,1)S(1)}, u32[]{:S(2)}, u32[]{:S(2)}) %collective-permute-start.47) | collective-permute-done | bytes 61472 | tf_op jit(solution)/shard_map/ppermute | solution.py:29
  187.9 7.4 %collective-permute-done.49.refs_1_ = bf16[224,768]{1,0:T(8,128)(2,1)S(1)} collective-permute-done((bf16[224,768]{1,0:T(8,128)(2,1)S(1)}, bf16[224,768]{1,0:T(8,128)(2,1)S(1)}, u32[]{:S(2)}, u32[]{:S(2)}) %collective-permute-start.49) | collective-permute-done | bytes 344096 | tf_op jit(solution)/shard_map/ppermute | solution.py:29
  195.3 4.3 %collective-permute-done.50.refs_2_ = bf16[224,768]{1,0:T(8,128)(2,1)S(1)} collective-permute-done((bf16[224,768]{1,0:T(8,128)(2,1)S(1)}, bf16[224,768]{1,0:T(8,128)(2,1)S(1)}, u32[]{:S(2)}, u32[]{:S(2)}) %collective-permute-start.50) | collective-permute-done | bytes 344096 | tf_op jit(solution)/shard_map/ppermute | solution.py:29
  213.3 6.6 %collective-permute-done.36.refs_1_ = bf16[128,768]{1,0:T(8,128)(2,1)S(1)} collective-permute-done((bf16[128,768]{1,0:T(8,128)(2,1)S(1)}, bf16[128,768]{1,0:T(8,128)(2,1)S(1)}, u32[]{:S(2)}, u32[]{:S(2)}) %collective-permute-start.36) | collective-permute-done | bytes 196640 | tf_op jit(solution)/shard_map/ppermute | solution.py:29
  219.9 8.2 %collective-permute-done.37.refs_2_ = bf16[128,768]{1,0:T(8,128)(2,1)S(1)} collective-permute-done((bf16[128,768]{1,0:T(8,128)(2,1)S(1)}, bf16[128,768]{1,0:T(8,128)(2,1)S(1)}, u32[]{:S(2)}, u32[]{:S(2)}) %collective-permute-start.37) | collective-permute-done | bytes 196640 | tf_op jit(solution)/shard_map/ppermute | solution.py:29
  231.8 3.3 %shard_map.297 = (f32[768,768]{1,0:T(8,128)}, f32[768,768]{1,0:T(8,128)}, f32[8,768]{1,0:T(8,128)S(1)}, f32[192,768]{1,0:T(8,128)}) custom-call(bf16[896,768]{1,0:T(8,128)(2,1)S(1)} %shard_map.296.mine_ref, bf16[896,768]{1,0:T(8,128)(2,1)S(1)} %collective-permute-done.52.other_ref), custom_call_target="tpu_custom_call" | custom-call | bytes 8085504 | tf_op jit(solution)/shard_map/pallas_call | solution.py:90
  (153 shorter events, 85.8 us)
Async XLA Ops:
  5.9 19.5 %collective-permute-start.1 = (bf16[152,768]{1,0:T(8,128)(2,1)S(1)}, bf16[152,768]{1,0:T(8,128)(2,1)S(1)}, u32[]{:S(2)}, u32[]{:S(2)}) collective-permute-start(bf16[152,768]{1,0:T(8,128)(2,1)S(1)} %shard_map.271.refs_0_.refs_10_), channel_id=1, source_target_pairs={{0,2},{1,3},{2,0},{3,1},{4,6},{5,7},{6,4},{7,5},{8,10},{9,11},{10,... | collective-permute-start | bytes 700424 | tf_op jit(solution)/shard_map/ppermute | solution.py:29
  8.5 16.9 %collective-permute-start.2 = (bf16[152,768]{1,0:T(8,128)(2,1)S(1)}, bf16[152,768]{1,0:T(8,128)(2,1)S(1)}, u32[]{:S(2)}, u32[]{:S(2)}) collective-permute-start(bf16[152,768]{1,0:T(8,128)(2,1)S(1)} %shard_map.271.refs_0_.refs_10_), channel_id=1, source_target_pairs={{0,3},{1,2},{2,1},{3,0},{4,7},{5,6},{6,5},{7,4},{8,11},{9,10},{10,... | collective-permute-start | bytes 700424 | tf_op jit(solution)/shard_map/ppermute | solution.py:29
  35.3 19.5 %collective-permute-start.14 = (bf16[128,768]{1,0:T(8,128)(2,1)S(1)}, bf16[128,768]{1,0:T(8,128)(2,1)S(1)}, u32[]{:S(2)}, u32[]{:S(2)}) collective-permute-start(bf16[128,768]{1,0:T(8,128)(2,1)S(1)} %shard_map.278.refs_0_.refs_5_), channel_id=1, source_target_pairs={{0,8},{4,12},{8,0},{12,4},{16,24},{20,28},{24,16},{28,20},{1,9},{5... | collective-permute-start | bytes 589832 | tf_op jit(solution)/shard_map/ppermute | solution.py:29
  60.0 32.0 %collective-permute-start.17 = (bf16[512,768]{1,0:T(8,128)(2,1)S(1)}, bf16[512,768]{1,0:T(8,128)(2,1)S(1)}, u32[]{:S(2)}, u32[]{:S(2)}) collective-permute-start(bf16[512,768]{1,0:T(8,128)(2,1)S(1)} %shard_map.279.refs_2_), channel_id=1, source_target_pairs={{0,4},{4,0},{8,12},{12,8},{16,20},{20,16},{24,28},{28,24},{1,5},{5... | collective-permute-start | bytes 2359304 | tf_op jit(solution)/shard_map/ppermute | solution.py:29
  66.1 25.9 %collective-permute-start.13 = (bf16[512,768]{1,0:T(8,128)(2,1)S(1)}, bf16[512,768]{1,0:T(8,128)(2,1)S(1)}, u32[]{:S(2)}, u32[]{:S(2)}) collective-permute-start(bf16[512,768]{1,0:T(8,128)(2,1)S(1)} %shard_map.277.refs_0_), channel_id=1, source_target_pairs={{0,4},{4,0},{8,12},{12,8},{16,20},{20,16},{24,28},{28,24},{1,5},{5... | collective-permute-start | bytes 2359304 | tf_op jit(solution)/shard_map/ppermute | solution.py:29
  67.0 15.9 %collective-permute-start.18 = (bf16[200,768]{1,0:T(8,128)(2,1)S(1)}, bf16[200,768]{1,0:T(8,128)(2,1)S(1)}, u32[]{:S(2)}, u32[]{:S(2)}) collective-permute-start(bf16[200,768]{1,0:T(8,128)(2,1)S(1)} %shard_map.280.refs_4_.refs_7_), channel_id=1, source_target_pairs={{0,1},{1,0},{2,3},{3,2},{4,5},{5,4},{6,7},{7,6},{8,9},{9,8},{10,11... | collective-permute-start | bytes 921608 | tf_op jit(solution)/shard_map/ppermute | solution.py:29
  67.7 24.3 %collective-permute-start.19 = (bf16[200,768]{1,0:T(8,128)(2,1)S(1)}, bf16[200,768]{1,0:T(8,128)(2,1)S(1)}, u32[]{:S(2)}, u32[]{:S(2)}) collective-permute-start(bf16[200,768]{1,0:T(8,128)(2,1)S(1)} %shard_map.280.refs_4_.refs_7_), channel_id=1, source_target_pairs={{0,2},{1,3},{2,0},{3,1},{4,6},{5,7},{6,4},{7,5},{8,10},{9,11},{10,... | collective-permute-start | bytes 921608 | tf_op jit(solution)/shard_map/ppermute | solution.py:29
  70.0 22.0 %collective-permute-start.20 = (bf16[200,768]{1,0:T(8,128)(2,1)S(1)}, bf16[200,768]{1,0:T(8,128)(2,1)S(1)}, u32[]{:S(2)}, u32[]{:S(2)}) collective-permute-start(bf16[200,768]{1,0:T(8,128)(2,1)S(1)} %shard_map.280.refs_4_.refs_7_), channel_id=1, source_target_pairs={{0,3},{1,2},{2,1},{3,0},{4,7},{5,6},{6,5},{7,4},{8,11},{9,10},{10,... | collective-permute-start | bytes 921608 | tf_op jit(solution)/shard_map/ppermute | solution.py:29
  112.6 19.2 %collective-permute-start.25 = (bf16[960,768]{1,0:T(8,128)(2,1)S(1)}, bf16[960,768]{1,0:T(8,128)(2,1)S(1)}, u32[]{:S(2)}, u32[]{:S(2)}) collective-permute-start(bf16[960,768]{1,0:T(8,128)(2,1)S(1)} %get-tuple-element.97), channel_id=1, source_target_pairs={{0,4},{4,0},{8,12},{12,8},{16,20},{20,16},{24,28},{28,24},{1,5},{5... | collective-permute-start | bytes 4423688 | tf_op jit(solution)/shard_map/ppermute | solution.py:29
  132.1 20.5 %collective-permute-start.26 = (bf16[240,768]{1,0:T(8,128)(2,1)S(1)}, bf16[240,768]{1,0:T(8,128)(2,1)S(1)}, u32[]{:S(2)}, u32[]{:S(2)}) collective-permute-start(bf16[240,768]{1,0:T(8,128)(2,1)S(1)} %get-tuple-element.99), channel_id=1, source_target_pairs={{0,8},{4,12},{8,0},{12,4},{16,24},{20,28},{24,16},{28,20},{1,9},{5... | collective-permute-start | bytes 1105928 | tf_op jit(solution)/shard_map/ppermute | solution.py:29
  135.7 14.8 %collective-permute-start.35 = (bf16[96,768]{1,0:T(8,128)(2,1)S(1)}, bf16[96,768]{1,0:T(8,128)(2,1)S(1)}, u32[]{:S(2)}, u32[]{:S(2)}) collective-permute-start(bf16[96,768]{1,0:T(8,128)(2,1)S(1)} %get-tuple-element.116), channel_id=1, source_target_pairs={{0,24},{4,28},{8,16},{12,20},{16,8},{20,12},{24,0},{28,4},{1,25},{... | collective-permute-start | bytes 442376 | tf_op jit(solution)/shard_map/ppermute | solution.py:29
  137.4 21.8 %collective-permute-start.27 = (bf16[240,768]{1,0:T(8,128)(2,1)S(1)}, bf16[240,768]{1,0:T(8,128)(2,1)S(1)}, u32[]{:S(2)}, u32[]{:S(2)}) collective-permute-start(bf16[240,768]{1,0:T(8,128)(2,1)S(1)} %get-tuple-element.100), channel_id=1, source_target_pairs={{0,16},{4,20},{8,24},{12,28},{16,0},{20,4},{24,8},{28,12},{1,17},{... | collective-permute-start | bytes 1105928 | tf_op jit(solution)/shard_map/ppermute | solution.py:29
  148.0 15.2 %collective-permute-start.43 = (bf16[200,768]{1,0:T(8,128)(2,1)S(1)}, bf16[200,768]{1,0:T(8,128)(2,1)S(1)}, u32[]{:S(2)}, u32[]{:S(2)}) collective-permute-start(bf16[200,768]{1,0:T(8,128)(2,1)S(1)} %get-tuple-element.126), channel_id=1, source_target_pairs={{0,1},{1,0},{2,3},{3,2},{4,5},{5,4},{6,7},{7,6},{8,9},{9,8},{10,11... | collective-permute-start | bytes 921608 | tf_op jit(solution)/shard_map/ppermute | solution.py:29
  150.5 26.8 %collective-permute-start.44 = (bf16[200,768]{1,0:T(8,128)(2,1)S(1)}, bf16[200,768]{1,0:T(8,128)(2,1)S(1)}, u32[]{:S(2)}, u32[]{:S(2)}) collective-permute-start(bf16[200,768]{1,0:T(8,128)(2,1)S(1)} %get-tuple-element.127), channel_id=1, source_target_pairs={{0,2},{1,3},{2,0},{3,1},{4,6},{5,7},{6,4},{7,5},{8,10},{9,11},{10,... | collective-permute-start | bytes 921608 | tf_op jit(solution)/shard_map/ppermute | solution.py:29
  152.6 24.8 %collective-permute-start.45 = (bf16[200,768]{1,0:T(8,128)(2,1)S(1)}, bf16[200,768]{1,0:T(8,128)(2,1)S(1)}, u32[]{:S(2)}, u32[]{:S(2)}) collective-permute-start(bf16[200,768]{1,0:T(8,128)(2,1)S(1)} %get-tuple-element.128), channel_id=1, source_target_pairs={{0,3},{1,2},{2,1},{3,0},{4,7},{5,6},{6,5},{7,4},{8,11},{9,10},{10,... | collective-permute-start | bytes 921608 | tf_op jit(solution)/shard_map/ppermute | solution.py:29
  160.6 16.7 %collective-permute-start.46 = (bf16[40,768]{1,0:T(8,128)(2,1)S(1)}, bf16[40,768]{1,0:T(8,128)(2,1)S(1)}, u32[]{:S(2)}, u32[]{:S(2)}) collective-permute-start(bf16[40,768]{1,0:T(8,128)(2,1)S(1)} %get-tuple-element.130), channel_id=1, source_target_pairs={{0,1},{1,0},{2,3},{3,2},{4,5},{5,4},{6,7},{7,6},{8,9},{9,8},{10,11... | collective-permute-start | bytes 184328 | tf_op jit(solution)/shard_map/ppermute | solution.py:29
  162.0 22.1 %collective-permute-start.47 = (bf16[40,768]{1,0:T(8,128)(2,1)S(1)}, bf16[40,768]{1,0:T(8,128)(2,1)S(1)}, u32[]{:S(2)}, u32[]{:S(2)}) collective-permute-start(bf16[40,768]{1,0:T(8,128)(2,1)S(1)} %get-tuple-element.131), channel_id=1, source_target_pairs={{0,2},{1,3},{2,0},{3,1},{4,6},{5,7},{6,4},{7,5},{8,10},{9,11},{10,... | collective-permute-start | bytes 184328 | tf_op jit(solution)/shard_map/ppermute | solution.py:29
  163.2 20.9 %collective-permute-start.48 = (bf16[40,768]{1,0:T(8,128)(2,1)S(1)}, bf16[40,768]{1,0:T(8,128)(2,1)S(1)}, u32[]{:S(2)}, u32[]{:S(2)}) collective-permute-start(bf16[40,768]{1,0:T(8,128)(2,1)S(1)} %get-tuple-element.132), channel_id=1, source_target_pairs={{0,3},{1,2},{2,1},{3,0},{4,7},{5,6},{6,5},{7,4},{8,11},{9,10},{10,... | collective-permute-start | bytes 184328 | tf_op jit(solution)/shard_map/ppermute | solution.py:29
  185.1 14.5 %collective-permute-start.50 = (bf16[224,768]{1,0:T(8,128)(2,1)S(1)}, bf16[224,768]{1,0:T(8,128)(2,1)S(1)}, u32[]{:S(2)}, u32[]{:S(2)}) collective-permute-start(bf16[224,768]{1,0:T(8,128)(2,1)S(1)} %get-tuple-element.133.refs_0_), channel_id=1, source_target_pairs={{0,16},{4,20},{8,24},{12,28},{16,0},{20,4},{24,8},{28,12},{1,17},{... | collective-permute-start | bytes 1032200 | tf_op jit(solution)/shard_map/ppermute | solution.py:29
  186.1 13.5 %collective-permute-start.51 = (bf16[224,768]{1,0:T(8,128)(2,1)S(1)}, bf16[224,768]{1,0:T(8,128)(2,1)S(1)}, u32[]{:S(2)}, u32[]{:S(2)}) collective-permute-start(bf16[224,768]{1,0:T(8,128)(2,1)S(1)} %get-tuple-element.133.refs_0_), channel_id=1, source_target_pairs={{0,24},{4,28},{8,16},{12,20},{16,8},{20,12},{24,0},{28,4},{1,25},{... | collective-permute-start | bytes 1032200 | tf_op jit(solution)/shard_map/ppermute | solution.py:29
  199.7 32.0 %collective-permute-start.52 = (bf16[896,768]{1,0:T(8,128)(2,1)S(1)}, bf16[896,768]{1,0:T(8,128)(2,1)S(1)}, u32[]{:S(2)}, u32[]{:S(2)}) collective-permute-start(bf16[896,768]{1,0:T(8,128)(2,1)S(1)} %shard_map.296.mine_ref), channel_id=1, source_target_pairs={{0,4},{4,0},{8,12},{12,8},{16,20},{20,16},{24,28},{28,24},{1,5},{5... | collective-permute-start | bytes 4128776 | tf_op jit(solution)/shard_map/ppermute | solution.py:29
  208.5 21.2 %collective-permute-start.42 = (bf16[288,768]{1,0:T(8,128)(2,1)S(1)}, bf16[288,768]{1,0:T(8,128)(2,1)S(1)}, u32[]{:S(2)}, u32[]{:S(2)}) collective-permute-start(bf16[288,768]{1,0:T(8,128)(2,1)S(1)} %shard_map.293.mine_ref), channel_id=1, source_target_pairs={{0,4},{4,0},{8,12},{12,8},{16,20},{20,16},{24,28},{28,24},{1,5},{5... | collective-permute-start | bytes 1327112 | tf_op jit(solution)/shard_map/ppermute | solution.py:29
  210.9 17.1 %collective-permute-start.37 = (bf16[128,768]{1,0:T(8,128)(2,1)S(1)}, bf16[128,768]{1,0:T(8,128)(2,1)S(1)}, u32[]{:S(2)}, u32[]{:S(2)}) collective-permute-start(bf16[128,768]{1,0:T(8,128)(2,1)S(1)} %get-tuple-element.121), channel_id=1, source_target_pairs={{0,2},{1,3},{2,0},{3,1},{4,6},{5,7},{6,4},{7,5},{8,10},{9,11},{10,... | collective-permute-start | bytes 589832 | tf_op jit(solution)/shard_map/ppermute | solution.py:29
  211.5 16.6 %collective-permute-start.38 = (bf16[128,768]{1,0:T(8,128)(2,1)S(1)}, bf16[128,768]{1,0:T(8,128)(2,1)S(1)}, u32[]{:S(2)}, u32[]{:S(2)}) collective-permute-start(bf16[128,768]{1,0:T(8,128)(2,1)S(1)} %get-tuple-element.122), channel_id=1, source_target_pairs={{0,3},{1,2},{2,1},{3,0},{4,7},{5,6},{6,5},{7,4},{8,11},{9,10},{10,... | collective-permute-start | bytes 589832 | tf_op jit(solution)/shard_map/ppermute | solution.py:29
  (46 other events, 602.0 us)

commit v2 on v1

--- a/solution.py
+++ b/solution.py
@@ -156,38 +156,44 @@
     return call(body, shape(rows * len(blocks), cols, blocks[0].dtype), blocks)
 
 
-def prepare_rows(block_input, w_out):
-    own, width = block_input.shape
-    cols = w_out.shape[0]
+def prepare_slice(w_out):
+    cols, width = w_out.shape
     inner = cols // plane_size()
 
-    def body(x_ref, w_ref, o_ref):
-        part = dot(one_hot(inner, cols, plane_index() * inner), w_ref[...], 1, 0)
-        o_ref[:own] = x_ref[...]
-        o_ref[own:] = part.astype(BF)
-
-    return call(body, shape(own + inner, width, BF), [block_input, w_out])
+    def body(w_ref, o_ref):
+        pick = one_hot(inner, cols, plane_index() * inner)
+        o_ref[...] = dot(pick, w_ref[...], 1, 0).astype(BF)
+
+    return call(body, shape(inner, width, BF), [w_out])
+
+
+def first_cut(units):
+    return units * 2 // 3 // 16 * 16
 
 
 def prepare_weights(w_up, w_down, b_up):
     hidden, width = w_down.shape
     units = hidden // plane_size()
     padded = -(-units // 128) * 128
-
-    def body(up_ref, down_ref, bias_ref, o_ref):
+    cut = first_cut(units)
+
+    def body(up_ref, down_ref, bias_ref, a_ref, b_ref):
         offset = plane_index() * units
         pick = one_hot(units, hidden, offset)
-        o_ref[:units] = dot(pick, up_ref[...], 1, 1).astype(BF)
-        o_ref[units : 2 * units] = dot(pick, down_ref[...], 1, 0).astype(BF)
+        up = dot(pick, up_ref[...], 1, 1).astype(BF)
+        a_ref[...] = up[:cut]
+        b_ref[: units - cut] = up[cut:]
+        at = 2 * units - cut
+        b_ref[units - cut : at] = dot(pick, down_ref[...], 1, 0).astype(BF)
         row = lax.broadcasted_iota(jnp.int32, (padded, hidden), 0)
         wide = jnp.where(row < units, one_hot(padded, hidden, offset).astype(F32), 0.0).astype(BF)
         bias = dot(three(bias_ref[...]).astype(BF), wide, 1, 1)
-        o_ref[2 * units :, :padded] = bias.astype(BF)
-        o_ref[2 * units :, padded:] = jnp.zeros((VEC, width - padded), BF)
+        b_ref[at:, :padded] = bias.astype(BF)
+        b_ref[at:, padded:] = jnp.zeros((VEC, width - padded), BF)
 
     return call(
-        body, shape(2 * units + VEC, width, BF), [w_up, w_down, b_up[None]],
-        flops=4 * units * hidden * width,
+        body, [shape(cut, width, BF), shape(2 * units - cut + VEC, width, BF)],
+        [w_up, w_down, b_up[None]], flops=4 * units * hidden * width,
     )
 
 
@@ -205,11 +211,11 @@
     return call(body, shape(own, width, BF), [lengths, cotangent], smem=1)
 
 
-def prepare_out(blocks, own, inner):
-    width = blocks[0].shape[1]
+def prepare_out(blocks):
+    inner, width = blocks[0].shape
 
     def body(*refs):
-        parts = [ref[own : own + inner].astype(F32) for ref in refs[:-1]]
+        parts = [ref[...].astype(F32) for ref in refs[:-1]]
         refs[-1][...] = jnp.concatenate(parts, axis=0).astype(BF)
 
     return call(body, shape(len(blocks) * inner, width, BF), list(blocks))
@@ -346,34 +352,36 @@
     return pl.BlockSpec((rows, cols), lambda i: (0, 0))
 
 
-def feed_forward(mine, other, mine_cot, other_cot, weights, own):
+def feed_forward(mine, other, mine_cot, other_cot, first, rest, own):
     width = mine.shape[1]
     steps = mine.shape[0] // own
-    nz = len(weights)
-    units = (weights[0].shape[0] - VEC) // 2
+    nz = len(first)
+    cut = first[0].shape[0]
+    units = (cut + rest[0].shape[0] - VEC) // 2
     padded = -(-units // 128) * 128
     hidden = nz * units
-    cot_rows = mine_cot.shape[0] // steps
 
     def body(*refs):
         x0, x1, c0, c1 = refs[:4]
-        w_refs = refs[4 : 4 + nz]
-        keep, send, act_ref, pre_ref, bg_ref, up, down, bias_ref = refs[4 + nz :]
+        a_refs, b_refs = refs[4 : 4 + nz], refs[4 + nz : 4 + 2 * nz]
+        keep, send, act_ref, pre_ref, bg_ref, up, down, bias_ref = refs[4 + 2 * nz :]
         step = pl.program_id(0)
 
         @pl.when(step == 0)
         def _():
             total = jnp.zeros((VEC, hidden), F32)
             for m in range(nz):
-                up[m * units : (m + 1) * units] = w_refs[m][:units]
-                down[m * units : (m + 1) * units] = w_refs[m][units : 2 * units]
-                place = one_hot(padded, hidden, m * units)
-                total = total + dot(w_refs[m][2 * units :, :padded], place, 1, 0)
+                at = m * units
+                up[at : at + cut] = a_refs[m][...]
+                up[at + cut : at + units] = b_refs[m][: units - cut]
+                down[at : at + units] = b_refs[m][units - cut : 2 * units - cut]
+                place = one_hot(padded, hidden, at)
+                total = total + dot(b_refs[m][2 * units - cut :, :padded], place, 1, 0)
             bias_ref[...] = jnp.broadcast_to(jnp.sum(total, axis=0, keepdims=True), (VEC, hidden))
             bg_ref[...] = jnp.zeros(bg_ref.shape, F32)
 
         rows = jnp.concatenate([x0[...], x1[...]], axis=0)
-        cot = jnp.concatenate([c0[:own], c1[:own]], axis=0)
+        cot = jnp.concatenate([c0[...], c1[...]], axis=0)
         values = dot(rows, up[...], 1, 1) + bias_ref[0:1]
         squared = values * values
         tangent = jnp.tanh(GELU_COEF * (values + GELU_CUBE * squared * values))
@@ -392,9 +400,8 @@
 
     n = 2 * steps * own
     return grid_call(
-        body, steps, [mine, other, mine_cot, other_cot, *weights],
-        [stepped(own, width)] * 2 + [stepped(cot_rows, width)] * 2
-        + [fixed(*weights[0].shape)] * nz,
+        body, steps, [mine, other, mine_cot, other_cot, *first, *rest],
+        [stepped(own, width)] * 4 + [fixed(*first[0].shape)] * nz + [fixed(*rest[0].shape)] * nz,
         [shape(n // 2, width, F32), shape(n // 2, width, BF), shape(n, hidden, BF),
          shape(n, hidden, BF), shape(VEC, hidden, F32)],
         [stepped(own, width)] * 2 + [stepped(2 * own, hidden)] * 2 + [fixed(VEC, hidden)],
@@ -404,32 +411,31 @@
     )
 
 
-def feed_forward_weights(mine, other, mine_cot, other_cot, weights, act, pre, bias_grad, own):
+def feed_forward_weights(mine, other, mine_cot, other_cot, rest, act, pre, bias_grad, own, units):
     width = mine.shape[1]
     steps = mine.shape[0] // own
-    nz = len(weights)
-    units = (weights[0].shape[0] - VEC) // 2
+    nz = len(rest)
     padded = -(-units // 128) * 128
     hidden = nz * units
-    cot_rows = mine_cot.shape[0] // steps
+    down_at = rest[0].shape[0] - VEC - units
 
     def body(*refs):
         x0, x1, c0, c1, act_ref, pre_ref, bg_ref = refs[:7]
         w_refs = refs[7 : 7 + nz]
         keep, send = refs[7 + nz : 9 + nz]
-        packs = refs[9 + nz : 9 + 2 * nz]
-        up_sum, down_sum, down = refs[9 + 2 * nz :]
+        downs, ups = refs[9 + nz : 9 + 2 * nz], refs[9 + 2 * nz : 9 + 3 * nz]
+        up_sum, down_sum, down = refs[9 + 3 * nz :]
         step = pl.program_id(0)
 
         @pl.when(step == 0)
         def _():
             for m in range(nz):
-                down[m * units : (m + 1) * units] = w_refs[m][units : 2 * units]
+                down[m * units : (m + 1) * units] = w_refs[m][down_at : down_at + units]
             up_sum[...] = jnp.zeros(up_sum.shape, F32)
             down_sum[...] = jnp.zeros(down_sum.shape, F32)
 
         rows = jnp.concatenate([x0[...], x1[...]], axis=0)
-        cot = jnp.concatenate([c0[:own], c1[:own]], axis=0)
+        cot = jnp.concatenate([c0[...], c1[...]], axis=0)
         up_sum[...] += dot(pre_ref[...], rows, 0, 0)
         down_sum[...] += dot(act_ref[...], cot, 0, 0)
         out = dot(act_ref[...], down[...], 1, 0)
@@ -440,30 +446,31 @@
         def _():
             bias_rows = three(bg_ref[0:1]).astype(BF)
             for m in range(nz):
-                kind = packs[m].dtype
+                kind = ups[m].dtype
                 part = slice(m * units, (m + 1) * units)
-                packs[m][:units] = up_sum[part].astype(kind)
-                packs[m][units : 2 * units] = down_sum[part].astype(kind)
+                ups[m][:units] = up_sum[part].astype(kind)
+                downs[m][...] = down_sum[part].astype(kind)
                 row = lax.broadcasted_iota(jnp.int32, (padded, hidden), 0)
                 place = one_hot(padded, hidden, m * units).astype(F32)
                 place = jnp.where(row < units, place, 0.0).astype(BF)
-                packs[m][2 * units :, :padded] = dot(bias_rows, place, 1, 1).astype(kind)
-                packs[m][2 * units :, padded:] = jnp.zeros((VEC, width - padded), kind)
+                ups[m][units:, :padded] = dot(bias_rows, place, 1, 1).astype(kind)
+                ups[m][units:, padded:] = jnp.zeros((VEC, width - padded), kind)
 
     n = 2 * steps * own
     outs = [shape(n // 2, width, F32), shape(n // 2, width, BF)]
-    outs += [shape(2 * units + VEC, width, F32 if m == 0 else BF) for m in range(nz)]
+    outs += [shape(units, width, F32 if m == 0 else BF) for m in range(nz)]
+    outs += [shape(units + VEC, width, F32 if m == 0 else BF) for m in range(nz)]
     out = grid_call(
-        body, steps, [mine, other, mine_cot, other_cot, act, pre, bias_grad, *weights],
-        [stepped(own, width)] * 2 + [stepped(cot_rows, width)] * 2
-        + [stepped(2 * own, hidden)] * 2 + [fixed(VEC, hidden)] + [fixed(*weights[0].shape)] * nz,
+        body, steps, [mine, other, mine_cot, other_cot, act, pre, bias_grad, *rest],
+        [stepped(own, width)] * 4 + [stepped(2 * own, hidden)] * 2 + [fixed(VEC, hidden)]
+        + [fixed(*rest[0].shape)] * nz,
         outs,
-        [stepped(own, width)] * 2 + [fixed(2 * units + VEC, width)] * nz,
+        [stepped(own, width)] * 2 + [fixed(units, width)] * nz + [fixed(units + VEC, width)] * nz,
         [pltpu.VMEM((hidden, width), F32), pltpu.VMEM((hidden, width), F32),
          pltpu.VMEM((hidden, width), BF)],
         6 * n * hidden * width,
     )
-    return out[0], out[1], out[2:]
+    return out[0], out[1], out[2 : 2 + nz], out[2 + nz :]
 
 
 def fold(keep, got, vec_at=None):
@@ -525,17 +532,17 @@
     return out[0], out[1], out[2], out[3:]
 
 
-def out_gradient(att, grad_res_bf, mlp_keep, mlp_send, vec):
+def out_gradient(att, grad_res_bf, vec):
     sub, nz = plane_size(), len(att)
     cols, own = att[0].shape
     width = vec.shape[1]
     inner = cols // sub
     grad_rows = nz * inner
-    rows = grad_rows + own + 2 * VEC
+    rows = grad_rows + 2 * VEC
     blocks = sub // 2
 
     def body(*refs):
-        g_ref, keep_in, send_in, vec_ref, keep, send, acc = refs[nz:]
+        g_ref, vec_ref, keep, send, acc = refs[nz:]
         for m in range(nz):
             acc[m * cols : (m + 1) * cols] = dot(refs[m][...], g_ref[...], 1, 0)
         p = plane_index()
@@ -543,46 +550,37 @@
         for core, ref in enumerate((keep, send)):
             for k in range(blocks):
                 j = p ^ (2 * k + core)
-                part = jnp.concatenate(
-                    [
-                        acc[pl.ds(pl.multiple_of(m * cols + j * inner, 8), inner)]
-                        for m in range(nz)
-                    ],
-                    axis=0,
-                )
-                at = k * rows
-                ref[at : at + grad_rows] = part.astype(ref.dtype)
-                source = keep_in if core == 0 else send_in
-                ref[at + grad_rows : at + grad_rows + own] = source[k * own : (k + 1) * own]
-                ref[at + grad_rows + own : at + rows] = jnp.concatenate([hi, low], axis=0).astype(
+                parts = [
+                    acc[pl.ds(pl.multiple_of(m * cols + j * inner, 8), inner)] for m in range(nz)
+                ]
+                ref[k * rows : (k + 1) * rows] = jnp.concatenate([*parts, hi, low], axis=0).astype(
                     ref.dtype
                 )
 
     return call(
         body, [shape(blocks * rows, width, F32), shape(blocks * rows, width, BF)],
-        [*att, grad_res_bf, mlp_keep, mlp_send, vec],
-        flops=2 * own * width * width,
+        [*att, grad_res_bf, vec], flops=2 * own * width * width,
         scratch=[pltpu.VMEM((nz * cols, width), F32)],
     )
 
 
-def block_result(parts, residual, b_down, late, lengths, nz):
+def block_result(parts, rows, residual, b_down, late, lengths, nz):
     own, width = residual.shape
     count = len(parts)
-    grad_rows = parts[0].shape[0] - own - 2 * VEC
-    inner = grad_rows // nz
+    at = parts[0].shape[0] - 2 * VEC
+    inner = at // nz
 
     def body(len_ref, *refs):
-        res_ref, b_ref, late_ref, out_ref = refs[count : count + 4]
-        packs = refs[count + 4 :]
-        total = total_of(refs[:count])
+        row_refs = refs[count : count + len(rows)]
+        res_ref, b_ref, late_ref, out_ref = refs[count + len(rows) : count + len(rows) + 4]
+        packs = refs[count + len(rows) + 4 :]
         length = jnp.int32(0)
         for i in range(len_ref.shape[1]):
             length = length + len_ref[0, i]
         slot = lax.axis_index("tensor") * own + lax.broadcasted_iota(jnp.int32, (own, width), 0)
-        final = res_ref[...] + total[grad_rows : grad_rows + own] + b_ref[...]
+        final = res_ref[...] + total_of(row_refs) + b_ref[...]
         out_ref[...] = jnp.where(slot < length, final, final * 0.0).astype(BF)
-        at = grad_rows + own
+        total = total_of(refs[:count])
         vec = total[at : at + VEC] + total[at + VEC : at + 2 * VEC]
         index = lax.broadcasted_iota(jnp.int32, (VEC, width), 0)
         for i in range(2):
@@ -594,26 +592,22 @@
 
     outs = [shape(own, width, BF)]
     outs += [shape(inner + 2 * VEC, width, F32 if m == 0 else BF) for m in range(nz)]
-    out = call(body, outs, [lengths, *parts, residual, b_down[None], late], smem=1)
+    out = call(body, outs, [lengths, *parts, *rows, residual, b_down[None], late], smem=1)
     return out[0], out[1:]
 
 
-def weight_sums(ffn, out):
-    count = len(ffn)
-    rows, width = ffn[0].shape
-    inner = out[0].shape[0] - 2 * VEC
+def weight_sums(downs, ups):
+    count = len(downs)
+    units, width = downs[0].shape
 
     def body(*refs):
-        pack_ref, vec_ref = refs[2 * count :]
-        total = total_of(refs[:count])
-        bias = jnp.sum(total[rows - VEC :], axis=0, keepdims=True)
-        other = total_of(refs[count : 2 * count])
-        vec_ref[...] = other[inner : inner + VEC] + other[inner + VEC :]
-        pack_ref[...] = jnp.concatenate(
-            [total[: rows - VEC], three(bias), other[:inner]], axis=0
+        up = total_of(refs[count : 2 * count])
+        bias = jnp.sum(up[units:], axis=0, keepdims=True)
+        refs[2 * count][...] = jnp.concatenate(
+            [up[:units], total_of(refs[:count]), three(bias)], axis=0
         ).astype(BF)
 
-    return call(body, [shape(rows + inner, width, BF), shape(VEC, width, F32)], [*ffn, *out])
+    return call(body, shape(2 * units + VEC, width, BF), [*downs, *ups])
 
 
 def attention_backward(lengths, qkv, logs, att, grad_att, blocks, w_t, own):
@@ -702,16 +696,32 @@
     )
 
 
-def joined_sums(parts, inner):
+def joined_sums(parts, out, joined_rows):
     width = parts[0].shape[1]
     count = len(parts)
+    inner = out[0].shape[0] - 2 * VEC
 
     def body(*refs):
         total = total_of(refs[:count])
-        refs[count][...] = total[:inner].astype(BF)
-        refs[count + 1][...] = total[inner : inner + VEC] + total[inner + VEC : inner + 2 * VEC]
-
-    return call(body, [shape(inner, width, BF), shape(VEC, width, F32)], list(parts))
+        other = total_of(refs[count : count + len(out)])
+        pack_ref, early_ref, late_ref = refs[count + len(out) :]
+        vec = other[inner : inner + VEC] + other[inner + VEC :]
+        early_ref[...] = vec
+        hi, low = two(vec)
+        late_ref[...] = (
+            total[joined_rows : joined_rows + VEC] + total[joined_rows + VEC : joined_rows + 2 * VEC]
+        )
+        tail = rows_of([hi[4:5], hi[5:6], low[4:5], low[5:6]], width)
+        pack_ref[...] = jnp.concatenate([total[:joined_rows], other[:inner], tail], axis=0).astype(
+            BF
+        )
+
+    return call(
+        body,
+        [shape(joined_rows + inner + VEC, width, BF), shape(VEC, width, F32),
+         shape(VEC, width, F32)],
+        [*parts, *out],
+    )
 
 
 def first_backward(parts, block_input, grad_res, gain):
@@ -727,16 +737,17 @@
     return call(body, shape(own, width, F32), [*parts, block_input, grad_res, gain[None]])
 
 
-def assemble_weights(mine, other, units, inner):
+def assemble_weights(mine, other, units):
     sub = plane_size()
     width = mine.shape[1]
     rows = mine.shape[0] // (sub // 2)
-    hidden, cols = sub * units, sub * inner
+    hidden = sub * units
     padded = -(-units // 128) * 128
 
-    def body(mine_ref, other_ref, up_ref, down_ref, bias_ref, out_ref, acc):
+    def body(mine_ref, other_ref, up_ref, down_ref, bias_ref, acc):
         p = plane_index()
         bias = jnp.zeros((VEC, hidden), F32)
+        row = lax.broadcasted_iota(jnp.int32, (padded, hidden), 0)
         for core, ref in enumerate((mine_ref, other_ref)):
             for k in range(sub // 2):
                 j = p ^ (2 * k + core)
@@ -744,39 +755,47 @@
                 part = ref[k * rows : (k + 1) * rows].astype(F32)
                 acc[pl.ds(at, units)] = part[:units]
                 down_ref[pl.ds(at, units)] = part[units : 2 * units]
-                place = one_hot(padded, hidden, at)
-                row = lax.broadcasted_iota(jnp.int32, (padded, hidden), 0)
-                place = jnp.where(row < units, place.astype(F32), 0.0).astype(BF)
-                tail = part[2 * units : 2 * units + VEC, :padded].astype(BF)
-                bias = bias + dot(tail, place, 1, 0)
-                out_ref[pl.ds(pl.multiple_of(j * inner, 8), inner)] = part[2 * units + VEC :]
-        bias_ref[...] = jnp.broadcast_to(jnp.sum(bias, axis=0, keepdims=True), (VEC, hidden))
+                place = jnp.where(row < units, one_hot(padded, hidden, at).astype(F32), 0.0)
+                tail = part[2 * units :, :padded].astype(BF)
+                bias = bias + dot(tail, place.astype(BF), 1, 0)
+        bias_ref[...] = jnp.sum(bias, axis=0, keepdims=True)
         up_ref[...] = jnp.transpose(acc[...])
 
     return call(
         body,
-        [shape(width, hidden, F32), shape(hidden, width, F32), shape(VEC, hidden, F32),
-         shape(cols, width, F32)],
+        [shape(width, hidden, F32), shape(hidden, width, F32), shape(1, hidden, F32)],
         [mine, other], scratch=[pltpu.VMEM((hidden, width), F32)],
     )
 
 
-def assemble_joined(mine, other):
+def assemble_joined(mine, other, joined_rows, inner):
     sub = plane_size()
     width = mine.shape[1]
-    inner = mine.shape[0] // (sub // 2)
-
-    def body(mine_ref, other_ref, out_ref):
+    rows = mine.shape[0] // (sub // 2)
+
+    def body(mine_ref, other_ref, joined_ref, out_ref, vec_ref):
         p = plane_index()
+        vec = jnp.zeros((VEC, width), F32)
         for core, ref in enumerate((mine_ref, other_ref)):
             whole = ref[...].astype(F32)
             for k in range(sub // 2):
                 j = p ^ (2 * k + core)
-                out_ref[pl.ds(pl.multiple_of(j * inner, 8), inner)] = whole[
-                    k * inner : (k + 1) * inner
+                part = whole[k * rows : (k + 1) * rows]
+                joined_ref[pl.ds(pl.multiple_of(j * joined_rows, 8), joined_rows)] = part[
+                    :joined_rows
                 ]
-
-    return call(body, shape(sub * inner, width, F32), [mine, other])
+                out_ref[pl.ds(pl.multiple_of(j * inner, 8), inner)] = part[
+                    joined_rows : joined_rows + inner
+                ]
+                vec = vec + part[joined_rows + inner :]
+        vec_ref[...] = vec[0:2] + vec[2:4]
+
+    return call(
+        body,
+        [shape(sub * joined_rows, width, F32), shape(sub * inner, width, F32),
+         shape(2, width, F32)],
+        [mine, other],
+    )
 
 
 def local(
@@ -804,18 +823,20 @@
     units = w_down.shape[0] // sub
     w_t = w_qkv.T
 
-    row_pack = prepare_rows(block_input, w_out)
-    row_blocks = [row_pack] + gather_z(row_pack)
+    row_blocks = [block_input] + gather_z(block_input)
+    out_slice = prepare_slice(w_out)
+    out_slices = [out_slice] + gather_z(out_slice)
     cot = prepare_cotangent(seq_lengths, cotangent)
     cot_mine, cot_other = gather_plane(cot)
-    weight_pack = prepare_weights(w_up, w_down, b_up)
-    out_mine, out_other = gather_plane(prepare_out(row_blocks, own, inner))
+    weights_a, weights_b = prepare_weights(w_up, w_down, b_up)
+    out_mine, out_other = gather_plane(prepare_out(out_slices))
+    first = [weights_a] + gather_z(weights_a)
 
     att_sent, qkv, rows_one, logs = attention_forward(
         seq_lengths, row_blocks, own, w_t, b_query, b_value, first_norm_gain, first_norm_bias
     )
     att = [att_sent[0]] + send_z(att_sent[1:])
-    weights = [weight_pack] + gather_z(weight_pack)
+    rest = [weights_b] + gather_z(weights_b)
     out_full = place_out(out_mine, out_other, inner, nz)
     residual, normed_two = middle(
         att, out_full, block_input, b_out, second_norm_gain, second_norm_bias
@@ -823,13 +844,15 @@
     mine, other = gather_plane(normed_two)
 
     keep, send, act, pre, bias_grad = feed_forward(
-        mine, other, cot_mine, cot_other, weights, own
+        mine, other, cot_mine, cot_other, first, rest, own
     )
     got = swap(send, "dp", 1)
-    mlp_keep, mlp_send, ffn_packs = feed_forward_weights(
-        mine, other, cot_mine, cot_other, weights, act, pre, bias_grad, own
+    mlp_keep, mlp_send, downs, ups = feed_forward_weights(
+        mine, other, cot_mine, cot_other, rest, act, pre, bias_grad, own, units
     )
     folded = fold(keep, got)
+    mlp_folded = fold(mlp_keep, swap(mlp_send, "dp", 1))
+    mlp_parts = [mlp_folded[0]] + send_plane(mlp_folded[1:])
     grad_res, grad_res_bf, early, grad_att_sent = second_backward(
         [folded[0]] + send_plane(folded[1:]), residual, cot, second_norm_gain, out_full, nz
     )
@@ -843,43 +866,44 @@
         [first_parts[0]] + first_got, block_input, grad_res, first_norm_gain
     )
 
+    joined_inner = joined.shape[0] // sub
     joined_keep, joined_send = joined_gradient(joined, rows_one, late)
-    joined_inner = joined.shape[0] // sub
     joined_folded = fold(joined_keep, swap(joined_send, "dp", 1), joined_inner)
-    joined_sum, late_sum = joined_sums(
-        [joined_folded[0]] + send_plane(joined_folded[1:]), joined_inner
-    )
-    grad_w_qkv = assemble_joined(*gather_plane(beyond(joined_sum).astype(BF))).T
-    bias_sum = beyond(late_sum)[2]
-
-    ffn_got = send_z(ffn_packs[1:])
-    out_keep, out_send = out_gradient(att, grad_res_bf, mlp_keep, mlp_send, early)
-    out_folded = fold(out_keep, swap(out_send, "dp", 1), nz * inner + own)
+    joined_parts = [joined_folded[0]] + send_plane(joined_folded[1:])
+    out_keep, out_send = out_gradient(att, grad_res_bf, early)
+    out_folded = fold(out_keep, swap(out_send, "dp", 1), nz * inner)
     block_output, out_packs = block_result(
-        [out_folded[0]] + send_plane(out_folded[1:]), residual, b_down, late_sum, seq_lengths, nz
-    )
-    out_got = send_z(out_packs[1:])
-    weight_pack_sum, early_sum = weight_sums(
-        [beyond(x) for x in [ffn_packs[0], *ffn_got]], [beyond(x) for x in [out_packs[0], *out_got]]
-    )
-    grad_w_up, grad_w_down, grad_b_up, grad_w_out = assemble_weights(
-        *gather_plane(weight_pack_sum), units, inner
-    )
-
+        [out_folded[0]] + send_plane(out_folded[1:]),
+        mlp_parts, residual, b_down, late, seq_lengths, nz,
+    )
+    out_parts = [out_packs[0]] + send_z(out_packs[1:])
+
+    downs = [downs[0]] + send_z(downs[1:])
+    ups = [ups[0]] + send_z(ups[1:])
+    weight_pack = weight_sums([beyond(x) for x in downs], [beyond(x) for x in ups])
+    grad_w_up, grad_w_down, grad_b_up = assemble_weights(*gather_plane(weight_pack), units)
+
+    joined_pack, early_sum, late_sum = joined_sums(
+        [beyond(x) for x in joined_parts], [beyond(x) for x in out_parts], joined_inner
+    )
+    grad_joined_t, grad_w_out, norm_sum = assemble_joined(
+        *gather_plane(joined_pack), joined_inner, inner
+    )
+    grad_w_qkv = grad_joined_t.T
     return (
         block_output,
         grad_input,
         grad_w_qkv,
-        bias_sum[:cols],
-        bias_sum[cols : 2 * cols],
+        late_sum[2, :cols],
+        late_sum[2, cols : 2 * cols],
         grad_w_out,
         early_sum[3],
         grad_w_up,
         grad_b_up[0],
         grad_w_down,
         early_sum[0],
-        early_sum[4],
-        early_sum[5],
+        norm_sum[0],
+        norm_sum[1],
         early_sum[1],
         early_sum[2],
     )

time: 237 us -> 238 us (level)
  starting transfers between devices: 69 us -> 84.3 us
  waiting for transfers between devices: 133 us -> 119 us
    ppermute x53 -> x66, starting transfers between devices: 69 us -> 84.3 us  [swap(): return lax.ppermute(x, axis, [(i, i ^ mask) for i in range(n)])]
    ppermute x53 -> x66, waiting for transfers between devices: 133 us -> 119 us  [swap(): return lax.ppermute(x, axis, [(i, i ^ mask) for i in range(n)])]
    pallas_call x25 -> x26, Pallas kernels: 21.4 us -> 21.3 us  [call(): pl.pallas_call(body, out_shape=outs, in_specs=given, out_specs=[pl.BlockS...]
  transfers between devices with their start and end apart: 53 -> 66, of which waited for: 28 -> 29; matrix products, arithmetic and copies ran while one was open for 1% -> 1% of each run, Pallas kernels for 8% -> 10%
where the time goes in v2:
time: 238 us; the launch traced here: 237 us
  waiting for transfers between devices  119 us (50%)
  starting transfers between devices  84.3 us (35%)
  Pallas kernels  28.7 us (12%)
  local copies, waits for them, and re-layouts  2.97 us (1%)
    ppermute x66, waiting for transfers between devices, swap(): return lax.ppermute(x, axis, [(i, i ^ mask) for i in range(n)])  119 us
    ppermute x66, starting transfers between devices, swap(): return lax.ppermute(x, axis, [(i, i ^ mask) for i in range(n)])  84.3 us
    pallas_call x26, Pallas kernels, call(): pl.pallas_call(body, out_shape=outs, in_specs=given, out_specs=[pl.BlockS...  21.3 us
    pallas_call x2, Pallas kernels, grid_call(): pl.pallas_call(body, grid=(steps,), in_specs=specs, out_specs=out_specs,...  7.48 us
  transfers between devices with their start and end apart: 66, of which 29 were waited for; matrix products, arithmetic and copies ran while one was open for 1% of the time, Pallas kernels for 10%

profile of v2, /device:TPU:0, one launch (start us, length us, event | category | flops | bytes accessed | tf_op | source)
XLA Modules:
  0.0 237.0 jit_solution(4387429038592782590)
XLA Ops:
  1.9 3.1 %collective-permute-start.6 = (bf16[24,768]{1,0:T(8,128)(2,1)S(1)}, bf16[24,768]{1,0:T(8,128)(2,1)S(1)}, u32[]{:S(2)}, u32[]{:S(2)}) collective-permute-start(bf16[24,768]{1,0:T(8,128)(2,1)S(1)} %shard_map.272.refs_0_), channel_id=1, source_target_pairs={{0,1},{1,0},{2,3},{3,2},{4,5},{5,4},{6,7},{7,6},{8,9},{9,8},{10,11... | collective-permute-start | bytes 110600 | tf_op jit(solution)/shard_map/ppermute | solution.py:29
  24.0 3.2 %collective-permute-start.2 = (bf16[128,768]{1,0:T(8,128)(2,1)S(1)}, bf16[128,768]{1,0:T(8,128)(2,1)S(1)}, u32[]{:S(2)}, u32[]{:S(2)}) collective-permute-start(bf16[128,768]{1,0:T(8,128)(2,1)S(1)} %copy-done.2), channel_id=1, source_target_pairs={{0,3},{1,2},{2,1},{3,0},{4,7},{5,6},{6,5},{7,4},{8,11},{9,10},{10,... | collective-permute-start | bytes 589832 | tf_op jit(solution)/shard_map/ppermute | solution.py:29
  28.3 4.1 %collective-permute-done.refs_1_.refs_11_ = bf16[128,768]{1,0:T(8,128)(2,1)S(1)} collective-permute-done((bf16[128,768]{1,0:T(8,128)(2,1)S(1)}, bf16[128,768]{1,0:T(8,128)(2,1)S(1)}, u32[]{:S(2)}, u32[]{:S(2)}) %collective-permute-start) | collective-permute-done | bytes 196640 | tf_op jit(solution)/shard_map/ppermute | solution.py:29
  32.4 7.7 %collective-permute-done.1.refs_2_.refs_12_ = bf16[128,768]{1,0:T(8,128)(2,1)S(1)} collective-permute-done((bf16[128,768]{1,0:T(8,128)(2,1)S(1)}, bf16[128,768]{1,0:T(8,128)(2,1)S(1)}, u32[]{:S(2)}, u32[]{:S(2)}) %collective-permute-start.1) | collective-permute-done | bytes 196640 | tf_op jit(solution)/shard_map/ppermute | solution.py:29
  40.1 3.7 %shard_map.271 = (bf16[192,128]{1,0:T(8,128)(2,1)S(1)}, bf16[192,128]{1,0:T(8,128)(2,1)S(1)}, bf16[192,128]{1,0:T(8,128)(2,1)S(1)}, bf16[192,128]{1,0:T(8,128)(2...) custom-call(s32[1,4]{1,0:T(1,128)S(1)} %copy-done.5, ...), custom_call_target="tpu_custom_call" | custom-call | flops 654311424 | bytes 3268112 | tf_op jit(solution)/shard_map/pallas_call | solution.py:90
  43.8 4.2 %collective-permute-start.3 = (bf16[192,128]{1,0:T(8,128)(2,1)S(1)}, bf16[192,128]{1,0:T(8,128)(2,1)S(1)}, u32[]{:S(2)}, u32[]{:S(2)}) collective-permute-start(bf16[192,128]{1,0:T(8,128)(2,1)S(1)} %get-tuple-element.89.refs_3_), channel_id=1, source_target_pairs={{0,1},{1,0},{2,3},{3,2},{4,5},{5,4},{6,7},{7,6},{8,9},{9,8},{10,11... | collective-permute-start | bytes 147464 | tf_op jit(solution)/shard_map/ppermute | solution.py:29
  58.3 6.3 %collective-permute-done.18.refs_2_ = bf16[128,768]{1,0:T(8,128)(2,1)S(1)} collective-permute-done((bf16[128,768]{1,0:T(8,128)(2,1)S(1)}, bf16[128,768]{1,0:T(8,128)(2,1)S(1)}, u32[]{:S(2)}, u32[]{:S(2)}) %collective-permute-start.18) | collective-permute-done | bytes 196640 | tf_op jit(solution)/shard_map/ppermute | solution.py:29
  64.8 4.1 %collective-permute-done.14.refs_2_ = bf16[128,768]{1,0:T(8,128)(2,1)S(1)} collective-permute-done((bf16[128,768]{1,0:T(8,128)(2,1)S(1)}, bf16[128,768]{1,0:T(8,128)(2,1)S(1)}, u32[]{:S(2)}, u32[]{:S(2)}) %collective-permute-start.14) | collective-permute-done | bytes 196640 | tf_op jit(solution)/shard_map/ppermute | solution.py:29
  76.3 5.1 %collective-permute-done.22.refs_6_ = bf16[64,768]{1,0:T(8,128)(2,1)S(1)} collective-permute-done((bf16[64,768]{1,0:T(8,128)(2,1)S(1)}, bf16[64,768]{1,0:T(8,128)(2,1)S(1)}, u32[]{:S(2)}, u32[]{:S(2)}) %collective-permute-start.22) | collective-permute-done | bytes 98336 | tf_op jit(solution)/shard_map/ppermute | solution.py:29
  85.9 11.7 %collective-permute-done.25.refs_10_.refs_9_ = bf16[136,768]{1,0:T(8,128)(2,1)S(1)} collective-permute-done((bf16[136,768]{1,0:T(8,128)(2,1)S(1)}, bf16[136,768]{1,0:T(8,128)(2,1)S(1)}, u32[]{:S(2)}, u32[]{:S(2)}) %collective-permute-start.25) | collective-permute-done | bytes 208928 | tf_op jit(solution)/shard_map/ppermute | solution.py:29
  97.6 3.9 %shard_map.281 = (f32[512,768]{1,0:T(8,128)S(1)}, bf16[512,768]{1,0:T(8,128)(2,1)S(1)}, bf16[1024,384]{1,0:T(8,128)(2,1)S(1)}, bf16[1024,384]{1,0:T(8,128)(2,1)S(1)}, f32[8,384]{1,0:T(8,128)S(1)}) custom-call(bf16[512,768]{1,0:T(8,128)(2,1)S(1)} %shard_map.277.refs_0_, bf16[512,768]{1,0:T(8,128)(2,1)S(1)} %collective-permute-done.16.refs_1_, ...), custom_call_target="tpu_custom_call" | custom-call | flops 1811939328 | bytes 8318976 | tf_op jit(solution)/shard_map/pallas_call | solution.py:340
  101.5 3.6 %shard_map.286 = (f32[512,768]{1,0:T(8,128)S(1)}, bf16[512,768]{1,0:T(8,128)(2,1)S(1)}, f32[96,768]{1,0:T(8,128)S(1)}, bf16[96,768]{1,0:T(8,128)(2,1)S(1)}, bf16...) custom-call(bf16[512,768]{1,0:T(8,128)(2,1)S(1)} %shard_map.277.refs, ...), custom_call_target="tpu_custom_call" | custom-call | flops 1811939328 | bytes 9461760 | tf_op jit(solution)/shard_map/pallas_call | solution.py:340
  105.2 4.3 %collective-permute-start.56 = (bf16[96,768]{1,0:T(8,128)(2,1)S(1)}, bf16[96,768]{1,0:T(8,128)(2,1)S(1)}, u32[]{:S(2)}, u32[]{:S(2)}) collective-permute-start(bf16[96,768]{1,0:T(8,128)(2,1)S(1)} %get-tuple-element.150), channel_id=1, source_target_pairs={{0,1},{1,0},{2,3},{3,2},{4,5},{5,4},{6,7},{7,6},{8,9},{9,8},{10,11... | collective-permute-start | bytes 442376 | tf_op jit(solution)/shard_map/ppermute | solution.py:29
  113.9 8.2 %collective-permute-done.57.refs_2_ = bf16[96,768]{1,0:T(8,128)(2,1)S(1)} collective-permute-done((bf16[96,768]{1,0:T(8,128)(2,1)S(1)}, bf16[96,768]{1,0:T(8,128)(2,1)S(1)}, u32[]{:S(2)}, u32[]{:S(2)}) %collective-permute-start.57) | collective-permute-done | bytes 147488 | tf_op jit(solution)/shard_map/ppermute | solution.py:29
  128.6 8.7 %collective-permute-done.58.refs_3_ = bf16[96,768]{1,0:T(8,128)(2,1)S(1)} collective-permute-done((bf16[96,768]{1,0:T(8,128)(2,1)S(1)}, bf16[96,768]{1,0:T(8,128)(2,1)S(1)}, u32[]{:S(2)}, u32[]{:S(2)}) %collective-permute-start.58) | collective-permute-done | bytes 147488 | tf_op jit(solution)/shard_map/ppermute | solution.py:29
  137.3 8.9 %collective-permute-start.39 = (bf16[192,128]{1,0:T(8,128)(2,1)S(1)}, bf16[192,128]{1,0:T(8,128)(2,1)S(1)}, u32[]{:S(2)}, u32[]{:S(2)}) collective-permute-start(bf16[192,128]{1,0:T(8,128)(2,1)S(1)} %get-tuple-element.122), channel_id=1, source_target_pairs={{0,1},{1,0},{2,3},{3,2},{4,5},{5,4},{6,7},{7,6},{8,9},{9,8},{10,11... | collective-permute-start | bytes 147464 | tf_op jit(solution)/shard_map/ppermute | solution.py:29
  155.0 4.7 %shard_map.288 = (f32[128,768]{1,0:T(8,128)S(1)}, bf16[128,768]{1,0:T(8,128)(2,1)S(1)}, bf16[128,768]{1,0:T(8,128)(2,1)S(1)}, bf16[128,768]{1,0:T(8,128)(2,1)S(1...) custom-call(s32[1,4]{1,0:T(1,128)S(1)} %copy-done.5, bf16[576,512]{1,0:T(8,128)(2,1)S(1)} %get-tuple-element.119.refs_0_, ...), custom_call_target="tpu_custom_call" | custom-call | flops 956301312 | bytes 4268048 | tf_op jit(solution)/shard_map/pallas_call | solution.py:90
  160.6 5.7 %collective-permute-done.63.refs_2_ = bf16[200,768]{1,0:T(8,128)(2,1)S(1)} collective-permute-done((bf16[200,768]{1,0:T(8,128)(2,1)S(1)}, bf16[200,768]{1,0:T(8,128)(2,1)S(1)}, u32[]{:S(2)}, u32[]{:S(2)}) %collective-permute-start.63) | collective-permute-done | bytes 307232 | tf_op jit(solution)/shard_map/ppermute | solution.py:29
  170.3 4.1 %collective-permute-done.36.refs_5_ = bf16[128,768]{1,0:T(8,128)(2,1)S(1)} collective-permute-done((bf16[128,768]{1,0:T(8,128)(2,1)S(1)}, bf16[128,768]{1,0:T(8,128)(2,1)S(1)}, u32[]{:S(2)}, u32[]{:S(2)}) %collective-permute-start.36) | collective-permute-done | bytes 196640 | tf_op jit(solution)/shard_map/ppermute | solution.py:29
  176.0 3.5 %collective-permute-done.37.refs_6_ = bf16[128,768]{1,0:T(8,128)(2,1)S(1)} collective-permute-done((bf16[128,768]{1,0:T(8,128)(2,1)S(1)}, bf16[128,768]{1,0:T(8,128)(2,1)S(1)}, u32[]{:S(2)}, u32[]{:S(2)}) %collective-permute-start.37) | collective-permute-done | bytes 196640 | tf_op jit(solution)/shard_map/ppermute | solution.py:29
  184.2 7.1 %collective-permute-done.33.refs_2_ = bf16[112,768]{1,0:T(8,128)(2,1)S(1)} collective-permute-done((bf16[112,768]{1,0:T(8,128)(2,1)S(1)}, bf16[112,768]{1,0:T(8,128)(2,1)S(1)}, u32[]{:S(2)}, u32[]{:S(2)}) %collective-permute-start.33) | collective-permute-done | bytes 172064 | tf_op jit(solution)/shard_map/ppermute | solution.py:29
  215.3 6.3 %collective-permute-done.42.refs_1_ = bf16[128,768]{1,0:T(8,128)(2,1)S(1)} collective-permute-done((bf16[128,768]{1,0:T(8,128)(2,1)S(1)}, bf16[128,768]{1,0:T(8,128)(2,1)S(1)}, u32[]{:S(2)}, u32[]{:S(2)}) %collective-permute-start.42) | collective-permute-done | bytes 196640 | tf_op jit(solution)/shard_map/ppermute | solution.py:29
  221.6 7.1 %collective-permute-done.43.refs_2_ = bf16[128,768]{1,0:T(8,128)(2,1)S(1)} collective-permute-done((bf16[128,768]{1,0:T(8,128)(2,1)S(1)}, bf16[128,768]{1,0:T(8,128)(2,1)S(1)}, u32[]{:S(2)}, u32[]{:S(2)}) %collective-permute-start.43) | collective-permute-done | bytes 196640 | tf_op jit(solution)/shard_map/ppermute | solution.py:29
  229.9 3.1 %shard_map.298 = (f32[768,768]{1,0:T(8,128)}, f32[768,768]{1,0:T(8,128)}, f32[1,768]{1,0:T(1,128)S(1)}) custom-call(bf16[800,768]{1,0:T(8,128)(2,1)S(1)} %shard_map.297.mine_ref, bf16[800,768]{1,0:T(8,128)(2,1)S(1)} %collective-permute-done.65.other_ref), custom_call_target="tpu_custom_call" | custom-call | bytes 7179264 | tf_op jit(solution)/shard_map/pallas_call | solution.py:90
  (179 shorter events, 103.5 us)
Async XLA Ops:
  22.7 27.8 %collective-permute-start.12 = (bf16[384,768]{1,0:T(8,128)(2,1)S(1)}, bf16[384,768]{1,0:T(8,128)(2,1)S(1)}, u32[]{:S(2)}, u32[]{:S(2)}) collective-permute-start(bf16[384,768]{1,0:T(8,128)(2,1)S(1)} %shard_map.274.mine_ref), channel_id=1, source_target_pairs={{0,4},{4,0},{8,12},{12,8},{16,20},{20,16},{24,28},{28,24},{1,5},{5... | collective-permute-start | bytes 1769480 | tf_op jit(solution)/shard_map/ppermute | solution.py:29
  22.8 17.2 %collective-permute-start.1 = (bf16[128,768]{1,0:T(8,128)(2,1)S(1)}, bf16[128,768]{1,0:T(8,128)(2,1)S(1)}, u32[]{:S(2)}, u32[]{:S(2)}) collective-permute-start(bf16[128,768]{1,0:T(8,128)(2,1)S(1)} %copy-done.2), channel_id=1, source_target_pairs={{0,2},{1,3},{2,0},{3,1},{4,6},{5,7},{6,4},{7,5},{8,10},{9,11},{10,... | collective-permute-start | bytes 589832 | tf_op jit(solution)/shard_map/ppermute | solution.py:29
  24.0 16.1 %collective-permute-start.2 = (bf16[128,768]{1,0:T(8,128)(2,1)S(1)}, bf16[128,768]{1,0:T(8,128)(2,1)S(1)}, u32[]{:S(2)}, u32[]{:S(2)}) collective-permute-start(bf16[128,768]{1,0:T(8,128)(2,1)S(1)} %copy-done.2), channel_id=1, source_target_pairs={{0,3},{1,2},{2,1},{3,0},{4,7},{5,6},{6,5},{7,4},{8,11},{9,10},{10,... | collective-permute-start | bytes 589832 | tf_op jit(solution)/shard_map/ppermute | solution.py:29
  27.8 28.3 %collective-permute-start.17 = (bf16[128,768]{1,0:T(8,128)(2,1)S(1)}, bf16[128,768]{1,0:T(8,128)(2,1)S(1)}, u32[]{:S(2)}, u32[]{:S(2)}) collective-permute-start(bf16[128,768]{1,0:T(8,128)(2,1)S(1)} %shard_map.278.refs_0_.refs_5_), channel_id=1, source_target_pairs={{0,8},{4,12},{8,0},{12,4},{16,24},{20,28},{24,16},{28,20},{1,9},{5... | collective-permute-start | bytes 589832 | tf_op jit(solution)/shard_map/ppermute | solution.py:29
  50.5 14.1 %collective-permute-start.18 = (bf16[128,768]{1,0:T(8,128)(2,1)S(1)}, bf16[128,768]{1,0:T(8,128)(2,1)S(1)}, u32[]{:S(2)}, u32[]{:S(2)}) collective-permute-start(bf16[128,768]{1,0:T(8,128)(2,1)S(1)} %shard_map.278.refs_0_.refs_5_), channel_id=1, source_target_pairs={{0,16},{4,20},{8,24},{12,28},{16,0},{20,4},{24,8},{28,12},{1,17},{... | collective-permute-start | bytes 589832 | tf_op jit(solution)/shard_map/ppermute | solution.py:29
  55.3 13.7 %collective-permute-start.14 = (bf16[128,768]{1,0:T(8,128)(2,1)S(1)}, bf16[128,768]{1,0:T(8,128)(2,1)S(1)}, u32[]{:S(2)}, u32[]{:S(2)}) collective-permute-start(bf16[128,768]{1,0:T(8,128)(2,1)S(1)} %get-tuple-element.92.refs_0_), channel_id=1, source_target_pairs={{0,16},{4,20},{8,24},{12,28},{16,0},{20,4},{24,8},{28,12},{1,17},{... | collective-permute-start | bytes 589832 | tf_op jit(solution)/shard_map/ppermute | solution.py:29
  64.7 32.9 %collective-permute-start.20 = (bf16[512,768]{1,0:T(8,128)(2,1)S(1)}, bf16[512,768]{1,0:T(8,128)(2,1)S(1)}, u32[]{:S(2)}, u32[]{:S(2)}) collective-permute-start(bf16[512,768]{1,0:T(8,128)(2,1)S(1)} %shard_map.279.refs_2_), channel_id=1, source_target_pairs={{0,4},{4,0},{8,12},{12,8},{16,20},{20,16},{24,28},{28,24},{1,5},{5... | collective-permute-start | bytes 2359304 | tf_op jit(solution)/shard_map/ppermute | solution.py:29
  69.0 28.6 %collective-permute-start.16 = (bf16[512,768]{1,0:T(8,128)(2,1)S(1)}, bf16[512,768]{1,0:T(8,128)(2,1)S(1)}, u32[]{:S(2)}, u32[]{:S(2)}) collective-permute-start(bf16[512,768]{1,0:T(8,128)(2,1)S(1)} %shard_map.277.refs_0_), channel_id=1, source_target_pairs={{0,4},{4,0},{8,12},{12,8},{16,20},{20,16},{24,28},{28,24},{1,5},{5... | collective-permute-start | bytes 2359304 | tf_op jit(solution)/shard_map/ppermute | solution.py:29
  81.4 16.2 %collective-permute-start.25 = (bf16[136,768]{1,0:T(8,128)(2,1)S(1)}, bf16[136,768]{1,0:T(8,128)(2,1)S(1)}, u32[]{:S(2)}, u32[]{:S(2)}) collective-permute-start(bf16[136,768]{1,0:T(8,128)(2,1)S(1)} %get-tuple-element.94.refs_8_.refs_7_), channel_id=1, source_target_pairs={{0,2},{1,3},{2,0},{3,1},{4,6},{5,7},{6,4},{7,5},{8,10},{9,11},{10,... | collective-permute-start | bytes 626696 | tf_op jit(solution)/shard_map/ppermute | solution.py:29
  81.4 16.2 %collective-permute-start.26 = (bf16[136,768]{1,0:T(8,128)(2,1)S(1)}, bf16[136,768]{1,0:T(8,128)(2,1)S(1)}, u32[]{:S(2)}, u32[]{:S(2)}) collective-permute-start(bf16[136,768]{1,0:T(8,128)(2,1)S(1)} %get-tuple-element.94.refs_8_.refs_7_), channel_id=1, source_target_pairs={{0,3},{1,2},{2,1},{3,0},{4,7},{5,6},{6,5},{7,4},{8,11},{9,10},{10,... | collective-permute-start | bytes 626696 | tf_op jit(solution)/shard_map/ppermute | solution.py:29
  110.1 13.8 %collective-permute-start.29 = (bf16[128,768]{1,0:T(8,128)(2,1)S(1)}, bf16[128,768]{1,0:T(8,128)(2,1)S(1)}, u32[]{:S(2)}, u32[]{:S(2)}) collective-permute-start(bf16[128,768]{1,0:T(8,128)(2,1)S(1)} %get-tuple-element.99), channel_id=1, source_target_pairs={{0,16},{4,20},{8,24},{12,28},{16,0},{20,4},{24,8},{28,12},{1,17},{... | collective-permute-start | bytes 589832 | tf_op jit(solution)/shard_map/ppermute | solution.py:29
  111.2 15.3 %collective-permute-start.30 = (bf16[128,768]{1,0:T(8,128)(2,1)S(1)}, bf16[128,768]{1,0:T(8,128)(2,1)S(1)}, u32[]{:S(2)}, u32[]{:S(2)}) collective-permute-start(bf16[128,768]{1,0:T(8,128)(2,1)S(1)} %get-tuple-element.100), channel_id=1, source_target_pairs={{0,24},{4,28},{8,16},{12,20},{16,8},{20,12},{24,0},{28,4},{1,25},{... | collective-permute-start | bytes 589832 | tf_op jit(solution)/shard_map/ppermute | solution.py:29
  113.9 52.5 %collective-permute-start.35 = (bf16[512,768]{1,0:T(8,128)(2,1)S(1)}, bf16[512,768]{1,0:T(8,128)(2,1)S(1)}, u32[]{:S(2)}, u32[]{:S(2)}) collective-permute-start(bf16[512,768]{1,0:T(8,128)(2,1)S(1)} %get-tuple-element.114), channel_id=1, source_target_pairs={{0,4},{4,0},{8,12},{12,8},{16,20},{20,16},{24,28},{28,24},{1,5},{5... | collective-permute-start | bytes 2359304 | tf_op jit(solution)/shard_map/ppermute | solution.py:29
  122.1 24.1 %collective-permute-start.59 = (bf16[104,768]{1,0:T(8,128)(2,1)S(1)}, bf16[104,768]{1,0:T(8,128)(2,1)S(1)}, u32[]{:S(2)}, u32[]{:S(2)}) collective-permute-start(bf16[104,768]{1,0:T(8,128)(2,1)S(1)} %get-tuple-element.154), channel_id=1, source_target_pairs={{0,1},{1,0},{2,3},{3,2},{4,5},{5,4},{6,7},{7,6},{8,9},{9,8},{10,11... | collective-permute-start | bytes 479240 | tf_op jit(solution)/shard_map/ppermute | solution.py:29
  122.1 24.1 %collective-permute-start.60 = (bf16[104,768]{1,0:T(8,128)(2,1)S(1)}, bf16[104,768]{1,0:T(8,128)(2,1)S(1)}, u32[]{:S(2)}, u32[]{:S(2)}) collective-permute-start(bf16[104,768]{1,0:T(8,128)(2,1)S(1)} %get-tuple-element.155), channel_id=1, source_target_pairs={{0,2},{1,3},{2,0},{3,1},{4,6},{5,7},{6,4},{7,5},{8,10},{9,11},{10,... | collective-permute-start | bytes 479240 | tf_op jit(solution)/shard_map/ppermute | solution.py:29
  123.9 22.3 %collective-permute-start.61 = (bf16[104,768]{1,0:T(8,128)(2,1)S(1)}, bf16[104,768]{1,0:T(8,128)(2,1)S(1)}, u32[]{:S(2)}, u32[]{:S(2)}) collective-permute-start(bf16[104,768]{1,0:T(8,128)(2,1)S(1)} %get-tuple-element.156), channel_id=1, source_target_pairs={{0,3},{1,2},{2,1},{3,0},{4,7},{5,6},{6,5},{7,4},{8,11},{9,10},{10,... | collective-permute-start | bytes 479240 | tf_op jit(solution)/shard_map/ppermute | solution.py:29
  146.4 14.1 %collective-permute-start.62 = (bf16[200,768]{1,0:T(8,128)(2,1)S(1)}, bf16[200,768]{1,0:T(8,128)(2,1)S(1)}, u32[]{:S(2)}, u32[]{:S(2)}) collective-permute-start(bf16[200,768]{1,0:T(8,128)(2,1)S(1)} %shard_map.296.refs_0_), channel_id=1, source_target_pairs={{0,8},{4,12},{8,0},{12,4},{16,24},{20,28},{24,16},{28,20},{1,9},{5... | collective-permute-start | bytes 921608 | tf_op jit(solution)/shard_map/ppermute | solution.py:29
  149.9 19.4 %collective-permute-start.31 = (bf16[448,768]{1,0:T(8,128)(2,1)S(1)}, bf16[448,768]{1,0:T(8,128)(2,1)S(1)}, u32[]{:S(2)}, u32[]{:S(2)}) collective-permute-start(bf16[448,768]{1,0:T(8,128)(2,1)S(1)} %get-tuple-element.105), channel_id=1, source_target_pairs={{0,4},{4,0},{8,12},{12,8},{16,20},{20,16},{24,28},{28,24},{1,5},{5... | collective-permute-start | bytes 2064392 | tf_op jit(solution)/shard_map/ppermute | solution.py:29
  151.9 14.3 %collective-permute-start.63 = (bf16[200,768]{1,0:T(8,128)(2,1)S(1)}, bf16[200,768]{1,0:T(8,128)(2,1)S(1)}, u32[]{:S(2)}, u32[]{:S(2)}) collective-permute-start(bf16[200,768]{1,0:T(8,128)(2,1)S(1)} %shard_map.296.refs_0_), channel_id=1, source_target_pairs={{0,16},{4,20},{8,24},{12,28},{16,0},{20,4},{24,8},{28,12},{1,17},{... | collective-permute-start | bytes 921608 | tf_op jit(solution)/shard_map/ppermute | solution.py:29
  160.5 20.0 %collective-permute-start.45 = (bf16[384,768]{1,0:T(8,128)(2,1)S(1)}, bf16[384,768]{1,0:T(8,128)(2,1)S(1)}, u32[]{:S(2)}, u32[]{:S(2)}) collective-permute-start(bf16[384,768]{1,0:T(8,128)(2,1)S(1)} %get-tuple-element.135), channel_id=1, source_target_pairs={{0,4},{4,0},{8,12},{12,8},{16,20},{20,16},{24,28},{28,24},{1,5},{5... | collective-permute-start | bytes 1769480 | tf_op jit(solution)/shard_map/ppermute | solution.py:29
  166.3 63.5 %collective-permute-start.65 = (bf16[800,768]{1,0:T(8,128)(2,1)S(1)}, bf16[800,768]{1,0:T(8,128)(2,1)S(1)}, u32[]{:S(2)}, u32[]{:S(2)}) collective-permute-start(bf16[800,768]{1,0:T(8,128)(2,1)S(1)} %shard_map.297.mine_ref), channel_id=1, source_target_pairs={{0,4},{4,0},{8,12},{12,8},{16,20},{20,16},{24,28},{28,24},{1,5},{5... | collective-permute-start | bytes 3686408 | tf_op jit(solution)/shard_map/ppermute | solution.py:29
  210.8 24.0 %collective-permute-start.55 = (bf16[416,768]{1,0:T(8,128)(2,1)S(1)}, bf16[416,768]{1,0:T(8,128)(2,1)S(1)}, u32[]{:S(2)}, u32[]{:S(2)}) collective-permute-start(bf16[416,768]{1,0:T(8,128)(2,1)S(1)} %shard_map.294.mine_ref), channel_id=1, source_target_pairs={{0,4},{4,0},{8,12},{12,8},{16,20},{20,16},{24,28},{28,24},{1,5},{5... | collective-permute-start | bytes 1916936 | tf_op jit(solution)/shard_map/ppermute | solution.py:29
  211.6 17.1 %collective-permute-start.43 = (bf16[128,768]{1,0:T(8,128)(2,1)S(1)}, bf16[128,768]{1,0:T(8,128)(2,1)S(1)}, u32[]{:S(2)}, u32[]{:S(2)}) collective-permute-start(bf16[128,768]{1,0:T(8,128)(2,1)S(1)} %get-tuple-element.129), channel_id=1, source_target_pairs={{0,2},{1,3},{2,0},{3,1},{4,6},{5,7},{6,4},{7,5},{8,10},{9,11},{10,... | collective-permute-start | bytes 589832 | tf_op jit(solution)/shard_map/ppermute | solution.py:29
  213.8 15.0 %collective-permute-start.44 = (bf16[128,768]{1,0:T(8,128)(2,1)S(1)}, bf16[128,768]{1,0:T(8,128)(2,1)S(1)}, u32[]{:S(2)}, u32[]{:S(2)}) collective-permute-start(bf16[128,768]{1,0:T(8,128)(2,1)S(1)} %get-tuple-element.130), channel_id=1, source_target_pairs={{0,3},{1,2},{2,1},{3,0},{4,7},{5,6},{6,5},{7,4},{8,11},{9,10},{10,... | collective-permute-start | bytes 589832 | tf_op jit(solution)/shard_map/ppermute | solution.py:29
  (58 other events, 752.3 us)
